TPU v7x, 32 devices: a whole 2x2x4 slice. The times are simulated.
32 devices in a mesh: seq: 8 (over y, x, core), tensor: 4 (over z).
Axes of the slice: x: 2, y: 2, z: 4, core: 2. Of those that a mesh axis runs over, the one named last changes fastest.
Arguments:
- queries: bfloat16 [8192, 8, 128], P('seq', 'tensor'), may hold values from -16 to 16
- keys: bfloat16 [8192, 128], P('seq'), may hold values from -6 to 6
- values: bfloat16 [8192, 128], P('seq'), may hold values from -6 to 6
- doc_ids: int32 [8192], P('seq'), may hold values from 0 to 7, never falling along the last dimension, each value on 1 to 4096 neighbouring positions
- w_query: bfloat16 [8, 128, 64], P('tensor'), may hold values from -0.5 to 0.5
- w_key: bfloat16 [128, 64], replicated, may hold values from -0.5 to 0.5
Outputs:
- student: bfloat16 [8192, 8, 128], P('seq', 'tensor')
- grad_wq: float32 [8, 128, 64], P('tensor')
- grad_key_weight: float32 [128, 64], replicated
- key_feature_grads: float32 [8192, 128], P('seq', 'tensor')
Inputs may be any that keep to these rules, and one draw needn't show every extreme that they name: `doc_ids`: document numbers never fall along the sequence and each number is used; each document has 1 to 4096 positions, and one has exactly 4096.
All inputs are finite; a program needn't handle non-finite values.
Results may differ from a plain program's by a relative error of at most 0.017.
Values may be sent and summed in bfloat16 or wider, within the bound.
No kernel may reach another device: no remote copies, remote signals or barrier semaphores. Data moves between devices by JAX's collectives and lax.ppermute only.
A program may use at most 64 MiB of HBM per device.

v0:
```python
import functools

import jax
import jax.numpy as jnp
from jax import lax
from jax.experimental import pallas as pl
from jax.experimental.pallas import tpu as pltpu
from jax.sharding import PartitionSpec as P


REACH = 4
NEG = -1e30
LOG2E = 1.4426950408889634
TQ = 256
TK = 1024
TC = 256
CH = 256
BF = jnp.bfloat16
F32 = jnp.float32

NT = (((1,), (1,)), ((), ()))
NN = (((1,), (0,)), ((), ()))


def mm(a, b, dims=NN):
    return lax.dot_general(a, b, dims, preferred_element_type=F32)


def feature_t(logits):
    top = jnp.max(logits, axis=0, keepdims=True)
    low = jnp.min(logits, axis=0, keepdims=True)
    up = jnp.exp(logits - top)
    down = jnp.exp(low - logits)
    up = up * (1.0 / jnp.sum(up, axis=0, keepdims=True))
    down = down * (1.0 / jnp.sum(down, axis=0, keepdims=True))
    return jnp.concatenate([up, down], axis=0)


def feature_back_t(feat, grad):
    half = feat.shape[0] // 2
    p, m = feat[:half], feat[half:]
    a, b = grad[:half], grad[half:]
    return p * (a - jnp.sum(a * p, axis=0, keepdims=True)) - m * (
        b - jnp.sum(b * m, axis=0, keepdims=True)
    )


def allowed_t(limit, first, start):
    j = lax.broadcasted_iota(jnp.int32, (limit, TQ), 0)
    i = lax.broadcasted_iota(jnp.int32, (1, TQ), 1) + first
    return (j <= i) & (j >= start)


def transposed(x):
    return x.astype(F32).T


def teacher_kernel(scale, q_ref, k_ref, v_ref, start_ref, vt_ref, acc_ref, stat_ref):
    n, width = k_ref.shape
    heads = q_ref.shape[1] // width
    vt_ref[...] = transposed(v_ref[...]).astype(BF)

    def head(h, carry):
        lane = pl.multiple_of(h * width, width)
        for qt in range(n // TQ):
            first = qt * TQ
            limit = first + TQ
            col = pl.ds(pl.multiple_of(h * n + first, TQ), TQ)
            q = q_ref[first:limit, pl.ds(lane, width)]
            ok = allowed_t(limit, first, start_ref[:, first:limit])
            s = jnp.where(ok, mm(k_ref[:limit], q, NT), NEG)
            top = jnp.max(s, axis=0, keepdims=True)
            w = jnp.exp2((s - top) * (scale * LOG2E))
            stat_ref[0:1, col] = top
            stat_ref[1:2, col] = jnp.sum(w, axis=0, keepdims=True)
            acc_ref[:, col] = mm(vt_ref[:, :limit], w.astype(BF))
        return carry

    lax.fori_loop(0, heads, head, 0)


def student_kernel(
    q_ref, k_ref, vt_ref, start_ref, wq_ref, wk_ref, qf_ref, kf_ref, num_ref, den_ref, kfb_ref
):
    n, width = k_ref.shape
    heads = q_ref.shape[1] // width
    kf = feature_t(mm(wk_ref[...], k_ref[...], NT))
    kf_ref[...] = kf
    kfb_ref[...] = kf.T.astype(BF)

    def head(h, carry):
        lane = pl.multiple_of(h * width, width)
        for qt in range(n // TQ):
            first = qt * TQ
            limit = first + TQ
            col = pl.ds(pl.multiple_of(h * n + first, TQ), TQ)
            q = q_ref[first:limit, pl.ds(lane, width)]
            ok = allowed_t(limit, first, start_ref[:, first:limit])
            qf = feature_t(mm(wq_ref[h], q, NT))
            qf_ref[:, col] = qf
            pr = jnp.where(ok, mm(kfb_ref[:limit], qf.astype(BF)), 0.0)
            den_ref[0:1, col] = jnp.sum(pr, axis=0, keepdims=True)
            num_ref[:, col] = mm(vt_ref[:, :limit], pr.astype(BF))
        return carry

    lax.fori_loop(0, heads, head, 0)


def load(src, slot, keys, values, codes, sem):
    n = keys.shape[0] // codes.shape[0]
    return (
        pltpu.make_async_copy(src.at[0:n], keys.at[slot * n : (slot + 1) * n], sem.at[slot, 0]),
        pltpu.make_async_copy(src.at[n : 2 * n], values.at[slot * n : (slot + 1) * n], sem.at[slot, 1]),
        pltpu.make_async_copy(src.at[2 * n : 2 * n + 16], codes.at[slot], sem.at[slot, 2]),
    )


def begin(copies):
    for c in copies:
        c.start()


def finish(copies):
    for c in copies:
        c.wait()


def matching(codes, code):
    return jnp.sum((codes[...].astype(F32) == code).astype(jnp.int32))


def window_part(
    scale, n, heads, begin_key, stop_key, lead_rows,
    q_ref, wk_ref, wink, winv, wkf, wvt, statet_ref, csum_ref,
    acc_ref, st2_ref, run_ref, racc_ref, sbuf_ref, smax_ref,
):
    width = wink.shape[1]
    tile0 = begin_key // TK
    tiles = stop_key // TK

    @pl.when(begin_key < stop_key)
    def _():
        def prepare(kt, carry):
            row = pl.ds(pl.multiple_of(kt * TK, TK), TK)
            kf = feature_t(mm(wk_ref[...], wink[row], NT))
            wkf[:, row] = kf
            j = lax.broadcasted_iota(jnp.int32, (1, TK), 1) + kt * TK
            kfm = jnp.where(j >= begin_key, kf, 0.0).astype(BF)
            vt = transposed(winv[row]).astype(BF)
            wvt[:, row] = vt
            statet_ref[...] += mm(vt, kfm, NT)
            part = kfm.astype(F32)
            for c in range(TK // 128):
                csum_ref[...] += part[:, c * 128 : (c + 1) * 128]
            return carry

        lax.fori_loop(tile0, tiles, prepare, 0)
        wq = max(TC, 2 * TC // heads)
        chains = [(h, c) for h in range(heads) for c in range(wq // TC)]
        factor = scale * LOG2E

        def qtile(qt, carry):
            first = pl.multiple_of(qt * wq, wq)

            def column(h, c):
                return pl.ds(pl.multiple_of(h * n + first + c * TC, TC), TC)

            for x, (h, c) in enumerate(chains):
                col = column(h, c)
                run_ref[x, 0:1] = st2_ref[0:1, col]
                run_ref[x, 1:2] = st2_ref[1:2, col]
                racc_ref[x] = acc_ref[:, col]

            def scores(x, kt, part, masked):
                h, c = chains[x]
                q = q_ref[pl.ds(first + c * TC, TC), h * width : (h + 1) * width]
                row = pl.multiple_of(kt * TK + part * CH, CH)
                s = mm(wink[pl.ds(row, CH)], q, NT)
                if masked:
                    j = lax.broadcasted_iota(jnp.int32, (CH, 1), 0) + row
                    s = jnp.where(j >= begin_key, s, NEG)
                sbuf_ref[x, part * CH : (part + 1) * CH] = s
                return jnp.max(s.reshape(CH // 8, 8, TC), axis=0)

            def stage(cur, kt, nxt, kt_nxt, masked):
                old = run_ref[cur, 0:1]
                new = jnp.maximum(old, jnp.max(smax_ref[cur], axis=0, keepdims=True))
                tops, sums, parts = [], [], []
                for part in range(TK // CH):
                    tops.append(scores(nxt, kt_nxt, part, masked))
                    w = jnp.exp2((sbuf_ref[cur, part * CH : (part + 1) * CH] - new) * factor)
                    sums.append(jnp.sum(w.reshape(CH // 8, 8, TC), axis=0))
                    parts.append(w.astype(BF))
                smax_ref[nxt] = functools.reduce(jnp.maximum, tops)
                f = jnp.exp2((old - new) * factor)
                total_w = jnp.sum(functools.reduce(jnp.add, sums), axis=0, keepdims=True)
                run_ref[cur, 0:1] = new
                run_ref[cur, 1:2] = run_ref[cur, 1:2] * f + total_w
                row = pl.ds(pl.multiple_of(kt * TK, TK), TK)
                racc_ref[cur] = racc_ref[cur] * f + mm(
                    wvt[:, row], jnp.concatenate(parts, axis=0)
                )

            def sweep(kt, masked):
                for x in range(len(chains) - 1):
                    stage(x, kt, x + 1, kt, masked)
                stage(len(chains) - 1, kt, 0, jnp.minimum(kt + 1, tiles - 1), False)

            smax_ref[0] = functools.reduce(
                jnp.maximum, [scores(0, tile0, part, True) for part in range(TK // CH)]
            )
            sweep(tile0, True)

            def step(kt, carry):
                sweep(kt, False)
                return carry

            lax.fori_loop(tile0 + 1, tiles, step, 0)
            i = lax.broadcasted_iota(jnp.int32, (1, wq), 1) + first
            live = i < lead_rows
            for x, (h, c) in enumerate(chains):
                col = column(h, c)
                ok = live[:, c * TC : (c + 1) * TC]
                st2_ref[0:2, col] = jnp.where(ok, run_ref[x, 0:2], st2_ref[0:2, col])
                acc_ref[:, col] = jnp.where(ok, racc_ref[x], acc_ref[:, col])
            return carry

        lax.fori_loop(0, (lead_rows + wq - 1) // wq, qtile, 0)


def window_kernel(
    scale,
    doc_ref, q_ref, start_ref, wk_ref, acc_in, stat_in, own_ref, two_ref, swap_two_ref,
    acc_ref, st2_ref, wkf, statet_ref, csum_ref,
    wink, winv, wcode, wvt, run_ref, racc_ref, sbuf_ref, smax_ref, sem,
):
    width = wk_ref.shape[1]
    n = start_ref.shape[1]
    heads = q_ref.shape[1] // width
    odd = lax.rem(lax.axis_index("seq"), 2)
    begin(load(two_ref, 1, wink, winv, wcode, sem))

    @pl.when(odd == 0)
    def _():
        begin(load(swap_two_ref, 2, wink, winv, wcode, sem))
        wcode[0] = jnp.zeros_like(wcode[0])

    @pl.when(odd == 1)
    def _():
        begin(load(own_ref, 2, wink, winv, wcode, sem))
        begin(load(swap_two_ref, 0, wink, winv, wcode, sem))

    acc_ref[...] = acc_in[...]
    st2_ref[...] = stat_in[...]
    statet_ref[...] = jnp.zeros_like(statet_ref)
    csum_ref[...] = jnp.zeros_like(csum_ref)
    lead_code = (doc_ref[0] + 1).astype(F32)
    lead_rows = jnp.sum((start_ref[...] == 0).astype(jnp.int32))
    finish(load(two_ref, 1, wink, winv, wcode, sem))
    finish(load(two_ref, 2, wink, winv, wcode, sem))

    @pl.when(odd == 1)
    def _():
        finish(load(two_ref, 0, wink, winv, wcode, sem))

    stop_key = wink.shape[0]
    window_part(
        scale, n, heads, stop_key - matching(wcode, lead_code), stop_key, lead_rows,
        q_ref, wk_ref, wink, winv, wkf, wvt, statet_ref, csum_ref,
        acc_ref, st2_ref, run_ref, racc_ref, sbuf_ref, smax_ref,
    )


def main_kernel(
    scale, grad_scale, back_scale, tensor_size,
    doc_ref, q_ref, k_ref, v_ref, start_ref, wk_ref,
    qf_ref, kf_ref, acc_in, num_ref, stat_in, den_ref, near_kf, statet_in, csum_in,
    two_ref, four_ref, own_ref, swap_two_ref, swap_four_ref,
    stu_ref, wq_ref, *rest,
):
    outs = rest[:tensor_size]
    (
        neark, nearv, nearc, wink, winv, wcode, wkf, wvt,
        gwq_ref, gwk_ref, adj_ref, adjs_ref, gkf_ref, gkf2_ref,
        state_ref, statet_ref, csum_ref, acc_ref, st2_ref, run_ref, racc_ref, sbuf_ref, smax_ref,
        near_sem, sem,
    ) = rest[tensor_size:]
    n, width = k_ref.shape
    heads = q_ref.shape[1] // width
    half = wk_ref.shape[0]
    odd = lax.rem(lax.axis_index("seq"), 2)
    begin(load(four_ref, 0, wink, winv, wcode, sem))
    begin(load(two_ref, 1, neark, nearv, nearc, near_sem))

    @pl.when(odd == 0)
    def _():
        begin(load(swap_four_ref, 1, wink, winv, wcode, sem))
        begin(load(swap_two_ref, 2, neark, nearv, nearc, near_sem))
        nearc[0] = jnp.zeros_like(nearc[0])

    @pl.when(odd == 1)
    def _():
        begin(load(own_ref, 2, neark, nearv, nearc, near_sem))
        begin(load(swap_two_ref, 0, neark, nearv, nearc, near_sem))
        wcode[1] = jnp.zeros_like(wcode[1])

    gkf2_ref[...] = jnp.zeros_like(gkf2_ref)
    gwq_ref[...] = jnp.zeros_like(gwq_ref)
    gwk_ref[...] = jnp.zeros_like(gwk_ref)
    adj_ref[...] = jnp.zeros_like(adj_ref)
    statet_ref[...] = statet_in[...]
    csum_ref[...] = csum_in[...]
    acc_ref[...] = acc_in[...]
    st2_ref[...] = stat_in[...]
    lead_code = (doc_ref[0] + 1).astype(F32)
    lead_rows = jnp.sum((start_ref[...] == 0).astype(jnp.int32))
    finish(load(four_ref, 0, wink, winv, wcode, sem))
    finish(load(two_ref, 1, neark, nearv, nearc, near_sem))
    finish(load(two_ref, 2, neark, nearv, nearc, near_sem))

    @pl.when(odd == 0)
    def _():
        finish(load(four_ref, 1, wink, winv, wcode, sem))

    @pl.when(odd == 1)
    def _():
        finish(load(two_ref, 0, neark, nearv, nearc, near_sem))

    near_stop = neark.shape[0]
    near_begin = near_stop - matching(nearc, lead_code)
    far_stop = jnp.where(odd == 1, n, 2 * n)
    far_begin = far_stop - matching(wcode, lead_code)
    linked = near_begin < near_stop
    window_part(
        scale, n, heads, far_begin, far_stop, lead_rows,
        q_ref, wk_ref, wink, winv, wkf, wvt, statet_ref, csum_ref,
        acc_ref, st2_ref, run_ref, racc_ref, sbuf_ref, smax_ref,
    )
    state_ref[...] = statet_ref[...].T
    csum_ref[...] = jnp.broadcast_to(
        jnp.sum(csum_ref[...], axis=1, keepdims=True), csum_ref.shape
    )

    link = linked.astype(F32)
    pad = lax.broadcasted_iota(jnp.int32, (n, 16), 1)
    v_aug = jnp.concatenate([v_ref[...], (pad < 2).astype(F32).astype(BF)], axis=1)
    statet_b = statet_ref[...].astype(BF)
    csum_b = csum_ref[:, :16].astype(BF)
    csum_b = jnp.where(pad[:width] < 2, csum_b.astype(F32), 0.0).astype(BF)
    state_aug = jnp.concatenate([state_ref[...].astype(BF), csum_b], axis=1)
    csum_row = jnp.sum(jnp.where(lax.broadcasted_iota(jnp.int32, csum_ref.shape, 1) == 0, csum_ref[...], 0.0).T, axis=0, keepdims=True)
    edge_row = lax.broadcasted_iota(jnp.int32, (16, width), 0)
    csum_hi = csum_row.astype(BF).astype(F32)
    csum_rows = jnp.where(edge_row == 0, csum_hi, jnp.where(edge_row == 1, csum_row - csum_hi, 0.0))
    statet_aug = jnp.concatenate([statet_b, csum_rows.astype(BF)], axis=0)
    kft_b = kf_ref[...].astype(BF)
    steps = [(qt, h) for qt in range(n // TQ) for h in range(heads)]
    held = {}

    def before(t):
        qt, h = steps[t]
        first = qt * TQ
        limit = first + TQ
        col = slice(h * n + first, h * n + limit)
        r = (start_ref[:, first:limit] == 0).astype(F32) * link
        qf = qf_ref[:, col]
        qf_b = qf.astype(BF)
        qf_r = (qf * r).astype(BF)
        carried = mm(statet_aug, qf_r)
        teacher = acc_ref[:, col] * (1.0 / st2_ref[1:2, col])
        inv = 1.0 / (den_ref[0:1, col] + carried[width : width + 1] + carried[width + 1 : width + 2])
        est = (num_ref[:, col] + carried[:width]) * inv
        stu_ref[first:limit, h * width : (h + 1) * width] = est.T.astype(BF)
        diff = est - teacher
        inv = inv * grad_scale
        gd = -jnp.sum(diff * est, axis=0, keepdims=True) * inv
        gd_hi = gd.astype(BF).astype(F32)
        row = lax.broadcasted_iota(jnp.int32, (16, TQ), 0)
        gd_rows = jnp.where(row == 0, gd_hi, jnp.where(row == 1, gd - gd_hi, 0.0))
        gn = diff * inv
        g = jnp.concatenate([gn.astype(BF), gd_rows.astype(BF)], axis=0)
        g_r = jnp.concatenate([(gn * r).astype(BF), (gd_rows * r).astype(BF)], axis=0)
        held[t] = (first, limit, h, qf_b, qf_r, g, g_r)

    def first_product(t):
        held[t] += (mm(v_aug[: held[t][1]], held[t][5]),)

    def second_product(t):
        first, limit, h, qf_b, qf_r, g, g_r, raw = held[t]
        start = start_ref[:, first:limit]
        j = lax.broadcasted_iota(jnp.int32, (TQ, TQ), 0) + first
        i = lax.broadcasted_iota(jnp.int32, (1, TQ), 1) + first
        gp = jnp.where((j <= i) & (j >= start), raw[first:], 0.0).astype(BF)
        if first:
            j = lax.broadcasted_iota(jnp.int32, (first, TQ), 0)
            gp = jnp.concatenate([jnp.where(j >= start, raw[:first], 0.0).astype(BF), gp], axis=0)
        gkf2_ref[:limit] += mm(gp, qf_b, NT)
        adj_ref[...] += mm(qf_r, g, NT)
        held[t] = (first, limit, h, mm(jnp.concatenate([kft_b[:, :limit], state_aug], axis=1), jnp.concatenate([gp, g_r], axis=0)))

    def after(t):
        first, limit, h, gq = held.pop(t)
        col = slice(h * n + first, h * n + limit)
        ga = feature_back_t(qf_ref[:, col], gq).astype(BF)
        gwq_ref[h] += mm(ga, q_ref[first:limit, h * width : (h + 1) * width])

    count = len(steps)
    before(0)
    first_product(0)
    for t in range(count):
        if t + 1 < count:
            before(t + 1)
            first_product(t + 1)
        second_product(t)
        if t:
            after(t - 1)
    after(count - 1)

    gkf = gkf2_ref[...].T
    gkf_ref[...] = gkf * back_scale
    gl = feature_back_t(kf_ref[...], gkf).astype(BF)
    gwk_ref[...] += mm(gl, k_ref[...])
    adj_b = adj_ref[:, :width].astype(BF)
    adjs_col = adj_ref[:, width : width + 1] + adj_ref[:, width + 1 : width + 2]

    def back_over(begin_key, stop_key, keys, values, feats):
        def back(kt, carry):
            row = pl.ds(pl.multiple_of(kt * TK, TK), TK)
            more = mm(adj_b, values[row], NT) + adjs_col
            j = lax.broadcasted_iota(jnp.int32, (1, TK), 1) + kt * TK
            gl = feature_back_t(feats[:, row], more)
            gl = jnp.where(j >= begin_key, gl, 0.0).astype(BF)
            gwk_ref[...] += mm(gl, keys[row])
            return carry

        lax.fori_loop(begin_key // TK, stop_key // TK, back, 0)

    back_over(near_begin, near_stop, neark, nearv, near_kf)
    back_over(far_begin, far_stop, wink, winv, wkf)

    for h in range(heads):
        wq_ref[h * half : (h + 1) * half] = gwq_ref[h].astype(BF)
    adjs_ref[...] = jnp.broadcast_to(adjs_col, adjs_ref.shape)
    row = jnp.max(adjs_ref[...].T, axis=0, keepdims=True)
    row_hi = row.astype(BF).astype(F32)
    tail = jnp.where(edge_row == 0, row_hi, jnp.where(edge_row == 1, row - row_hi, 0.0)).astype(BF)
    gwk_b = gwk_ref[...].astype(BF)
    tensor = len(outs)
    rows = width // tensor
    mine = lax.axis_index("tensor")
    for k in range(tensor):
        piece = pl.ds(pl.multiple_of(lax.rem(mine + k, tensor) * rows, rows), rows)
        outs[k][0:rows] = gkf_ref[piece].astype(BF)
        part = adj_ref[piece, :width].astype(BF)
        blocks = [part[c * 16 : (c + 1) * 16] for c in range(rows // 16)] + [tail]
        blocks += [gwk_b[c * 16 : (c + 1) * 16] for c in range(half // 16)]
        outs[k][rows:] = jnp.zeros_like(outs[k][rows:])
        for c, block in enumerate(blocks):
            outs[k][rows:, c * width : (c + 1) * width] = block


def join_kernel(tensor, doc_ref, wq_ref, *refs):
    ins, (sum_ref, out_ref) = refs[:tensor], refs[tensor:]
    rows = sum_ref.shape[0]
    width = out_ref.shape[1]
    half = width // 2
    total = ins[0][...].astype(F32)
    for k in range(1, tensor):
        total = total + ins[k][...].astype(F32)
    sum_ref[...] = total[:rows]
    at = wq_ref.shape[0]
    out_ref[0:at] = wq_ref[...]
    pieces = [total[rows:, c * width : (c + 1) * width] for c in range(total.shape[1] // width)]
    parts = rows // 16
    out_ref[at : at + rows] = jnp.concatenate(pieces[:parts], axis=0).astype(BF)
    at += rows
    tail = pieces[parts]
    row = tail[0:1] + tail[1:2]
    row_hi = row.astype(BF).astype(F32)
    index = lax.broadcasted_iota(jnp.int32, (16, width), 0)
    code = (doc_ref[0] + 1).astype(F32)
    tail = jnp.where(index == 0, row_hi, jnp.where(index == 1, row - row_hi, code))
    out_ref[at : at + 16] = tail.astype(BF)
    at += 16
    gwk = jnp.concatenate(pieces[parts + 1 : parts + 1 + half // 16], axis=0)
    hi = gwk.astype(BF)
    out_ref[at : at + half] = hi
    out_ref[at + half : at + 2 * half] = (gwk - hi.astype(F32)).astype(BF)


def last_kernel(
    seq, back_scale,
    doc_ref, edge_ref, gath_ref, sum_ref, v_ref,
    kfg_ref, gwq_ref, gwk_ref,
    adj_ref, adjs_ref, col_ref,
):
    n, width = v_ref.shape
    heads, half = gwq_ref.shape[:2]
    rows = sum_ref.shape[0]
    me = lax.axis_index("seq")
    mine = lax.axis_index("tensor")
    last_code = (doc_ref[n - 1] + 1).astype(F32)
    edge = edge_ref[n - 1]

    def gathered(first, size):
        x = gath_ref[0, first : first + size].astype(F32)
        for d in range(1, seq):
            x = x + gath_ref[d, first : first + size].astype(F32)
        return x

    for h in range(heads):
        gwq_ref[h] = gathered(h * half, half)
    at = heads * half
    gwk_ref[...] = gathered(at + rows + 16, half) + gathered(at + rows + 16 + half, half)
    adj_ref[...] = jnp.zeros_like(adj_ref)
    adjs_ref[...] = jnp.zeros_like(adjs_ref)

    def later(s, carry):
        a = gath_ref[s, at : at + rows].astype(F32)
        t = gath_ref[s, at + rows : at + rows + 16].astype(F32)
        same = t[2:3] == last_code
        adj_ref[...] += jnp.where(same, a, 0.0)
        adjs_ref[...] += jnp.where(same, t[0:1] + t[1:2], 0.0)
        return carry

    lax.fori_loop(me + 1, jnp.minimum(me + REACH + 1, seq), later, 0)
    adj = adj_ref[...]
    a_hi = adj.astype(BF)
    a_lo = (adj - a_hi.astype(F32)).astype(BF)
    col_ref[...] = jnp.broadcast_to(adjs_ref[...], (width, width)).T
    col = col_ref[pl.ds(pl.multiple_of(mine * rows, rows), rows), 0:1]
    j = lax.broadcasted_iota(jnp.int32, (1, n), 1)
    more = mm(a_hi, v_ref[...], NT) + mm(a_lo, v_ref[...], NT) + col
    kfg_ref[...] = sum_ref[...] + jnp.where(j >= edge, more, 0.0) * back_scale


VM = pl.BlockSpec(memory_space=pltpu.VMEM)
SM = pl.BlockSpec(memory_space=pltpu.SMEM)
ANY = pl.BlockSpec(memory_space=pl.ANY)


def grant(mib):
    return pltpu.CompilerParams(vmem_limit_bytes=mib << 20)


def cost(flops, size):
    return pl.CostEstimate(flops=flops, bytes_accessed=size, transcendentals=0)


def shards(queries, keys, values, doc_ids, w_query, w_key):
    n, heads, width = queries.shape
    half = w_key.shape[1]
    seq = lax.axis_size("seq")
    tensor = lax.axis_size("tensor")
    scale = width ** (-0.5)
    everyone = range(seq)
    assert n // width <= 16 and n // width * 16 == width

    codes = (doc_ids + 1).astype(BF).reshape(n // width, width)
    codes = jnp.pad(codes, ((0, 16 - n // width), (0, 0)))
    pack = jnp.concatenate([keys, values, codes], axis=0)

    def hop(x, distance):
        return lax.ppermute(x, "seq", [(i, i + distance) for i in everyone if i + distance < seq])

    two = hop(pack, 2)
    own = lax.ppermute(pack, "seq", [(i, i + 1) for i in everyone if i % 2 == 0])

    qs = queries.reshape(n, heads * width)
    starts = jnp.sum((doc_ids[None, :] < doc_ids[:, None]).astype(jnp.int32), axis=1)
    start_row = starts.reshape(1, n)
    wq_t = jnp.transpose(w_query, (0, 2, 1))
    wk_t = w_key.T
    sds = jax.ShapeDtypeStruct
    cols = heads * n
    rows = width // tensor
    near = REACH - 1
    chains = max(heads, 2)
    square = sds((width, width), F32)
    wide = sds((width, cols), F32)
    flat = sds((8, cols), F32)
    scan = [
        pltpu.VMEM((chains, 8, TC), F32),
        pltpu.VMEM((chains, width, TC), F32),
        pltpu.VMEM((chains, TK, TC), F32),
        pltpu.VMEM((chains, 8, TC), F32),
    ]
    vt, acc, stat = pl.pallas_call(
        functools.partial(teacher_kernel, scale),
        out_shape=(sds((width, n), BF), wide, flat),
        in_specs=[VM] * 4,
        out_specs=[VM] * 3,
        compiler_params=grant(12),
        cost_estimate=cost(4 * n * n * width * heads, 4 << 20),
    )(qs, keys, values, start_row)
    four = hop(pack, 4)
    qf, kf, num, den = pl.pallas_call(
        student_kernel,
        out_shape=(wide, sds((width, n), F32), wide, flat),
        in_specs=[VM] * 6,
        out_specs=[VM] * 4,
        scratch_shapes=[pltpu.VMEM((n, width), BF)],
        compiler_params=grant(12),
        cost_estimate=cost(4 * n * n * width * heads, 4 << 20),
    )(qs, keys, vt, start_row, wq_t, wk_t)

    swap_two = lax.ppermute(two, "seq", [(i, i ^ 1) for i in everyone])
    acc, stat, near_kf, statet, csum = pl.pallas_call(
        functools.partial(window_kernel, scale),
        out_shape=(wide, flat, sds((width, near * n), F32), square, square),
        in_specs=[SM] + [VM] * 5 + [ANY] * 3,
        out_specs=[VM] * 5,
        scratch_shapes=[
            pltpu.VMEM((near * n, width), BF),
            pltpu.VMEM((near * n, width), BF),
            pltpu.VMEM((near, 16, width), BF),
            pltpu.VMEM((width, near * n), BF),
        ]
        + scan
        + [pltpu.SemaphoreType.DMA((near, 3))],
        compiler_params=grant(20),
        cost_estimate=cost(8 * n * n * width * heads, 4 << 20),
    )(doc_ids, qs, start_row, wk_t, acc, stat, own, two, swap_two)

    swap_four = lax.ppermute(four, "seq", [(i, i - 1) for i in everyone if i % 2 == 1])
    student, wq_part, *pieces = pl.pallas_call(
        functools.partial(main_kernel, scale, 2.0 / (n * seq), float(n * seq), tensor),
        out_shape=[sds((n, heads * width), BF), sds((heads * half, width), BF)]
        + [sds((rows + 16, n), BF)] * tensor,
        in_specs=[SM] + [VM] * 14 + [ANY] * 5,
        out_specs=[VM] * (2 + tensor),
        scratch_shapes=[
            pltpu.VMEM((near * n, width), BF),
            pltpu.VMEM((near * n, width), BF),
            pltpu.VMEM((near, 16, width), BF),
            pltpu.VMEM((2 * n, width), BF),
            pltpu.VMEM((2 * n, width), BF),
            pltpu.VMEM((2, 16, width), BF),
            pltpu.VMEM((width, 2 * n), F32),
            pltpu.VMEM((width, 2 * n), BF),
            pltpu.VMEM((heads, half, width), F32),
            pltpu.VMEM((half, width), F32),
            pltpu.VMEM((width, width + 16), F32),
            pltpu.VMEM((width, 128), F32),
            pltpu.VMEM((width, n), F32),
            pltpu.VMEM((n, width), F32),
            pltpu.VMEM((width, width), F32),
            pltpu.VMEM((width, width), F32),
            pltpu.VMEM((width, 128), F32),
            pltpu.VMEM((width, cols), F32),
            pltpu.VMEM((8, cols), F32),
        ]
        + scan
        + [pltpu.SemaphoreType.DMA((near, 3)), pltpu.SemaphoreType.DMA((2, 3))],
        compiler_params=grant(32),
        cost_estimate=cost(16 * n * n * width * heads, 8 << 20),
    )(
        doc_ids, qs, keys, values, start_row, wk_t,
        qf, kf, acc, num, stat, den, near_kf, statet, csum,
        two, four, own, swap_two, swap_four,
    )

    arrived = [pieces[0]]
    for k in range(1, tensor):
        arrived.append(
            lax.ppermute(pieces[k], "tensor", [(i, (i + k) % tensor) for i in range(tensor)])
        )
    packed = heads * half + rows + 16 + 2 * half
    part, out = pl.pallas_call(
        functools.partial(join_kernel, tensor),
        out_shape=(sds((rows, n), F32), sds((packed, width), BF)),
        in_specs=[SM] + [VM] * (tensor + 1),
        out_specs=[VM] * 2,
        compiler_params=grant(8),
        cost_estimate=cost(n * width, 1 << 20),
    )(doc_ids, wq_part, *arrived)
    gathered = lax.all_gather(out, "seq")
    key_grads, gwq, gwk = pl.pallas_call(
        functools.partial(last_kernel, seq, float(n * seq)),
        out_shape=(sds((rows, n), F32), sds((heads, half, width), F32), sds((half, width), F32)),
        in_specs=[SM, SM, VM, VM, VM],
        out_specs=[VM] * 3,
        scratch_shapes=[
            pltpu.VMEM((rows, width), F32),
            pltpu.VMEM((1, width), F32),
            pltpu.VMEM((width, width), F32),
        ],
        compiler_params=grant(12),
        cost_estimate=cost(4 * n * width * width, 2 << 20),
    )(doc_ids, starts, gathered, part, values)
    return student.reshape(n, heads, width), jnp.transpose(gwq, (0, 2, 1)), gwk.T, key_grads.T


def solution(mesh):
    placed = (
        P("seq", "tensor", None),
        P("seq", None),
        P("seq", None),
        P("seq"),
        P("tensor", None, None),
        P(),
    )

    return jax.shard_map(
        shards,
        mesh=mesh,
        in_specs=placed,
        out_specs=(P("seq", "tensor", None), P("tensor", None, None), P(), P("seq", "tensor")),
        check_vma=False,
    )
```

profile of v0, /device:TPU:0, one launch (start us, length us, event | category | flops | bytes accessed | tf_op | source)
XLA Modules:
  0.0 77.9 jit_solution(10575873609826024173)
XLA Ops:
  0.7 0.8 fusion.2
  1.4 1.1 %fusion.1 = bf16[2064,128]{1,0:T(8,128)(2,1)S(1)} fusion(bf16[8,128]{1,0:T(8,128)(2,1)S(1)} %fusion.2, bf16[1024,128]{1,0:T(8,128)(2,1)} %v_ref.5, bf16[1024,128]{1,0:T(8,128)(2,1)} %k_ref.5), kind=kLoop, calls=%fused_computation.3 | loop fusion | flops 2113536 | bytes 1054720 | tf_op jit(solution)/shard_map/concatenate | solution.py:561
  2.5 4.9 %collective-permute-start.1 = (bf16[2064,128]{1,0:T(8,128)(2,1)S(1)}, bf16[2064,128]{1,0:T(8,128)(2,1)S(1)}, u32[]{:S(2)}, u32[]{:S(2)}) collective-permute-start(bf16[2064,128]{1,0:T(8,128)(2,1)S(1)} %fusion.1), channel_id=1, source_target_pairs={{0,8},{4,12},{8,16},{12,20},{16,24},{20,28},{1,9},{5,13},{9,17},{1... | collective-permute-start | bytes 1585160 | tf_op jit(solution)/shard_map/ppermute | solution.py:564
  7.4 3.4 %collective-permute-start.3 = (bf16[2064,128]{1,0:T(8,128)(2,1)S(1)}, bf16[2064,128]{1,0:T(8,128)(2,1)S(1)}, u32[]{:S(2)}, u32[]{:S(2)}) collective-permute-start(bf16[2064,128]{1,0:T(8,128)(2,1)S(1)} %fusion.1), channel_id=1, source_target_pairs={{0,16},{4,20},{8,24},{12,28},{1,17},{5,21},{9,25},{13,29},{2,18},{... | collective-permute-start | bytes 1585160 | tf_op jit(solution)/shard_map/ppermute | solution.py:564
  10.9 1.3 %collective-permute-start = (bf16[2064,128]{1,0:T(8,128)(2,1)S(1)}, bf16[2064,128]{1,0:T(8,128)(2,1)S(1)}, u32[]{:S(2)}, u32[]{:S(2)}) collective-permute-start(bf16[2064,128]{1,0:T(8,128)(2,1)S(1)} %fusion.1), channel_id=1, source_target_pairs={{0,4},{8,12},{16,20},{24,28},{1,5},{9,13},{17,21},{25,29},{2,6},{1... | collective-permute-start | bytes 1585160 | tf_op jit(solution)/shard_map/ppermute | solution.py:567
  12.2 6.5 %collective-permute-done.1.two_ref = bf16[2064,128]{1,0:T(8,128)(2,1)S(1)} collective-permute-done((bf16[2064,128]{1,0:T(8,128)(2,1)S(1)}, bf16[2064,128]{1,0:T(8,128)(2,1)S(1)}, u32[]{:S(2)}, u32[]{:S(2)}) %collective-permute-start.1) | collective-permute-done | bytes 528416 | tf_op jit(solution)/shard_map/ppermute | solution.py:564
  18.7 0.0 collective-permute-start.2
  18.7 0.1 copy.12
  18.8 12.2 %collective-permute-done.3.four_ref = bf16[2064,128]{1,0:T(8,128)(2,1)S(1)} collective-permute-done((bf16[2064,128]{1,0:T(8,128)(2,1)S(1)}, bf16[2064,128]{1,0:T(8,128)(2,1)S(1)}, u32[]{:S(2)}, u32[]{:S(2)}) %collective-permute-start.3) | collective-permute-done | bytes 528416 | tf_op jit(solution)/shard_map/ppermute | solution.py:564
  30.9 1.3 %collective-permute-start.4 = (bf16[2064,128]{1,0:T(8,128)(2,1)S(1)}, bf16[2064,128]{1,0:T(8,128)(2,1)S(1)}, u32[]{:S(2)}, u32[]{:S(2)}) collective-permute-start(bf16[2064,128]{1,0:T(8,128)(2,1)S(1)} %collective-permute-done.3.four_ref), channel_id=1, source_target_pairs={{4,0},{12,8},{20,16},{28,24},{5,1},{13,9},{21,17},{29,25},{6,2},{1... | collective-permute-start | bytes 1585160 | tf_op jit(solution)/shard_map/ppermute | solution.py:625
  32.2 0.6 convert_reduce_fusion.edge_ref
  32.8 0.0 copy-done
  32.8 0.0 copy-done.1
  32.8 0.0 copy-start.3
  32.8 0.0 copy-start.4
  32.8 3.8 %shard_map.93 = (bf16[128,1024]{1,0:T(8,128)(2,1)S(1)}, f32[128,2048]{1,0:T(8,128)S(1)}, f32[8,2048]{1,0:T(8,128)S(1)}) custom-call(bf16[1024,256]{1,0:T(8,128)(2,1)S(1)} %bitcast.14, bf16[1024,128]{1,0:T(8,128)(2,1)S(1)} %copy-done.1, bf16[1024,128]{1,0:T(8,128)(2,1)S(1)} %copy-done, s32[1,1024]{1,0:T(1,128)S(1)} %bitcast.18), custom_call_target="tpu_custom_call" | custom-call | flops 1073741824 | bytes 4194304 | tf_op jit(solution)/shard_map/pallas_call | solution.py:588
  36.7 4.9 %shard_map.94 = (f32[128,2048]{1,0:T(8,128)S(1)}, f32[128,1024]{1,0:T(8,128)S(1)}, f32[128,2048]{1,0:T(8,128)S(1)}, f32[8,2048]{1,0:T(8,128)S(1)}) custom-call(bf16[1024,256]{1,0:T(8,128)(2,1)S(1)} %bitcast.15, bf16[1024,128]{1,0:T(8,128)(2,1)S(1)} %copy-done.1, bf16[128,1024]{1,0:T(8,128)(2,1)S(1)} %get-tuple-element.27.vt_ref, s32[1,1024]{1,0:T(1,128)S(1)} %bitcast.19, ...), custom_call_target="tpu_custom_call" | custom-call | flops 1073741824 | bytes 4194304 | tf_op jit(solution)/shard_map/pallas_call | solution.py:597
  41.6 0.0 collective-permute-done.own_ref
  41.6 0.0 collective-permute-done.2.swap_two_ref
  41.6 1.1 %shard_map.95 = (f32[128,2048]{1,0:T(8,128)S(1)}, f32[8,2048]{1,0:T(8,128)S(1)}, f32[128,3072]{1,0:T(8,128)S(1)}, f32[128,128]{1,0:T(8,128)S(1)}, f32[128,128]{1,0:T(8,128)S(1)}) custom-call(s32[1024]{0:T(1024)S(1)} %copy-done.2, bf16[1024,256]{1,0:T(8,128)(2,1)S(1)} %bitcast.16, s32[1,1024]{1,0:T(1,128)S(1)} %bitcast.20, bf16[64,128]{1,0:T(8,128)(2,1)S(1)} %bitcast.24, ...), custom_call_target="tpu_custom_call" | custom-call | flops 2147483648 | bytes 4194304 | tf_op jit(solution)/shard_map/pallas_call | solution.py:608
  42.7 0.0 collective-permute-done.4.swap_four_ref
  42.7 5.5 %shard_map.96 = (bf16[1024,256]{1,0:T(8,128)(2,1)S(1)}, bf16[128,128]{1,0:T(8,128)(2,1)S(1)}, bf16[48,1024]{1,0:T(8,128)(2,1)S(1)}, bf16[48,1024]{1,0:T(8,128)(2...) custom-call(s32[1024]{0:T(1024)S(1)} %copy-done.2, bf16[1024,256]{1,0:T(8,128)(2,1)S(1)} %bitcast.17, ...), custom_call_target="tpu_custom_call" | custom-call | flops 4294967296 | bytes 8388608 | tf_op jit(solution)/shard_map/pallas_call | solution.py:626
  48.2 1.6 %collective-permute-start.5 = (bf16[48,1024]{1,0:T(8,128)(2,1)S(1)}, bf16[48,1024]{1,0:T(8,128)(2,1)S(1)}, u32[]{:S(2)}, u32[]{:S(2)}) collective-permute-start(bf16[48,1024]{1,0:T(8,128)(2,1)S(1)} %get-tuple-element.42), channel_id=1, source_target_pairs={{0,1},{1,2},{2,3},{3,0},{4,5},{5,6},{6,7},{7,4},{8,9},{9,10},{10,1... | collective-permute-start | bytes 294920 | tf_op jit(solution)/shard_map/ppermute | solution.py:666
  49.8 2.6 %collective-permute-start.6 = (bf16[48,1024]{1,0:T(8,128)(2,1)S(1)}, bf16[48,1024]{1,0:T(8,128)(2,1)S(1)}, u32[]{:S(2)}, u32[]{:S(2)}) collective-permute-start(bf16[48,1024]{1,0:T(8,128)(2,1)S(1)} %get-tuple-element.43), channel_id=1, source_target_pairs={{0,2},{1,3},{2,0},{3,1},{4,6},{5,7},{6,4},{7,5},{8,10},{9,11},{10,... | collective-permute-start | bytes 294920 | tf_op jit(solution)/shard_map/ppermute | solution.py:666
  52.4 1.3 %collective-permute-start.7 = (bf16[48,1024]{1,0:T(8,128)(2,1)S(1)}, bf16[48,1024]{1,0:T(8,128)(2,1)S(1)}, u32[]{:S(2)}, u32[]{:S(2)}) collective-permute-start(bf16[48,1024]{1,0:T(8,128)(2,1)S(1)} %get-tuple-element.44), channel_id=1, source_target_pairs={{0,3},{1,0},{2,1},{3,2},{4,7},{5,4},{6,5},{7,6},{8,11},{9,8},{10,9... | collective-permute-start | bytes 294920 | tf_op jit(solution)/shard_map/ppermute | solution.py:666
  53.8 0.9 %reshape.25 = bf16[1024,2,128]{2,1,0:T(2,128)(2,1)} reshape(bf16[1024,256]{1,0:T(8,128)(2,1)S(1)} %get-tuple-element.39) | data formatting | bytes 1048576 | tf_op jit(solution)/shard_map/reshape | solution.py:691
  54.7 0.0 collective-permute-done.5.refs_1_
  54.7 2.2 %collective-permute-done.6.refs_2_ = bf16[48,1024]{1,0:T(8,128)(2,1)S(1)} collective-permute-done((bf16[48,1024]{1,0:T(8,128)(2,1)S(1)}, bf16[48,1024]{1,0:T(8,128)(2,1)S(1)}, u32[]{:S(2)}, u32[]{:S(2)}) %collective-permute-start.6) | collective-permute-done | bytes 98336 | tf_op jit(solution)/shard_map/ppermute | solution.py:666
  56.9 1.1 %collective-permute-done.7.refs_3_ = bf16[48,1024]{1,0:T(8,128)(2,1)S(1)} collective-permute-done((bf16[48,1024]{1,0:T(8,128)(2,1)S(1)}, bf16[48,1024]{1,0:T(8,128)(2,1)S(1)}, u32[]{:S(2)}, u32[]{:S(2)}) %collective-permute-start.7) | collective-permute-done | bytes 98336 | tf_op jit(solution)/shard_map/ppermute | solution.py:666
  58.0 0.7 shard_map.97
  58.6 17.5 %all-gather = bf16[2432,128]{1,0:T(8,128)(2,1)S(1)} all-gather(bf16[304,128]{1,0:T(8,128)(2,1)S(1)} %get-tuple-element.45), channel_id=2, replica_groups=mesh['seq'=8,'tensor'=4] {'seq'}, dimensions={0}, use_global_device_ids=true | all-gather | bytes 700416 | tf_op jit(solution)/shard_map/all_gather | solution.py:677
  76.2 1.7 %shard_map.98 = (f32[32,1024]{1,0:T(8,128)}, f32[2,64,128]{2,1,0:T(8,128)}, f32[64,128]{1,0:T(8,128)}) custom-call(s32[1024]{0:T(1024)S(1)} %copy-done.2, s32[1024]{0:T(1024)S(1)} %convert_reduce_fusion.edge_ref, bf16[8,304,128]{2,1,0:T(8,128)(2,1)S(1)} %bitcast.13, f32[32,1024]{1,0:T(8,128)S(1)} %get-tuple-element.46.sum_ref, bf16[1024,128]{1,0:T(8,128)(2,1)S(1)} %copy-done), custom_call_target="tpu_custom_call" | custom-call | flops 67108864 | bytes 2097152 | tf_op jit(solution)/shard_map/pallas_call | solution.py:678
  (8 shorter events, 0.0 us)
Async XLA Ops:
  0.6 31.6 %copy-start.2 = (s32[1024]{0:T(1024)S(1)}, s32[1024]{0:T(1024)}, u32[]{:S(2)}) copy-start(s32[1024]{0:T(1024)} %doc_ref.7) | copy-start | bytes 12292
  0.6 18.0 %copy-start.5 = (bf16[1024,2,128]{2,1,0:T(2,128)(2,1)S(1)}, bf16[1024,2,128]{2,1,0:T(2,128)(2,1)}, u32[]{:S(2)}) copy-start(bf16[1024,2,128]{2,1,0:T(2,128)(2,1)} %param.6) | copy-start | bytes 1572868
  1.4 31.4 %copy-start = (bf16[1024,128]{1,0:T(8,128)(2,1)S(1)}, bf16[1024,128]{1,0:T(8,128)(2,1)}, u32[]{:S(2)}) copy-start(bf16[1024,128]{1,0:T(8,128)(2,1)} %v_ref.5) | copy-start | bytes 786436
  1.4 31.4 %copy-start.1 = (bf16[1024,128]{1,0:T(8,128)(2,1)S(1)}, bf16[1024,128]{1,0:T(8,128)(2,1)}, u32[]{:S(2)}) copy-start(bf16[1024,128]{1,0:T(8,128)(2,1)} %k_ref.5) | copy-start | bytes 786436
  2.5 16.1 %collective-permute-start.1 = (bf16[2064,128]{1,0:T(8,128)(2,1)S(1)}, bf16[2064,128]{1,0:T(8,128)(2,1)S(1)}, u32[]{:S(2)}, u32[]{:S(2)}) collective-permute-start(bf16[2064,128]{1,0:T(8,128)(2,1)S(1)} %fusion.1), channel_id=1, source_target_pairs={{0,8},{4,12},{8,16},{12,20},{16,24},{20,28},{1,9},{5,13},{9,17},{1... | collective-permute-start | bytes 1585160 | tf_op jit(solution)/shard_map/ppermute | solution.py:564
  7.4 23.5 %collective-permute-start.3 = (bf16[2064,128]{1,0:T(8,128)(2,1)S(1)}, bf16[2064,128]{1,0:T(8,128)(2,1)S(1)}, u32[]{:S(2)}, u32[]{:S(2)}) collective-permute-start(bf16[2064,128]{1,0:T(8,128)(2,1)S(1)} %fusion.1), channel_id=1, source_target_pairs={{0,16},{4,20},{8,24},{12,28},{1,17},{5,21},{9,25},{13,29},{2,18},{... | collective-permute-start | bytes 1585160 | tf_op jit(solution)/shard_map/ppermute | solution.py:564
  10.9 30.7 %collective-permute-start = (bf16[2064,128]{1,0:T(8,128)(2,1)S(1)}, bf16[2064,128]{1,0:T(8,128)(2,1)S(1)}, u32[]{:S(2)}, u32[]{:S(2)}) collective-permute-start(bf16[2064,128]{1,0:T(8,128)(2,1)S(1)} %fusion.1), channel_id=1, source_target_pairs={{0,4},{8,12},{16,20},{24,28},{1,5},{9,13},{17,21},{25,29},{2,6},{1... | collective-permute-start | bytes 1585160 | tf_op jit(solution)/shard_map/ppermute | solution.py:567
  18.7 22.9 %collective-permute-start.2 = (bf16[2064,128]{1,0:T(8,128)(2,1)S(1)}, bf16[2064,128]{1,0:T(8,128)(2,1)S(1)}, u32[]{:S(2)}, u32[]{:S(2)}) collective-permute-start(bf16[2064,128]{1,0:T(8,128)(2,1)S(1)} %collective-permute-done.1.two_ref), channel_id=1, source_target_pairs={{0,4},{4,0},{8,12},{12,8},{16,20},{20,16},{24,28},{28,24},{1,5},{5... | collective-permute-start | bytes 1585160 | tf_op jit(solution)/shard_map/ppermute | solution.py:607
  30.9 11.7 %collective-permute-start.4 = (bf16[2064,128]{1,0:T(8,128)(2,1)S(1)}, bf16[2064,128]{1,0:T(8,128)(2,1)S(1)}, u32[]{:S(2)}, u32[]{:S(2)}) collective-permute-start(bf16[2064,128]{1,0:T(8,128)(2,1)S(1)} %collective-permute-done.3.four_ref), channel_id=1, source_target_pairs={{4,0},{12,8},{20,16},{28,24},{5,1},{13,9},{21,17},{29,25},{6,2},{1... | collective-permute-start | bytes 1585160 | tf_op jit(solution)/shard_map/ppermute | solution.py:625
  32.8 3.9 %copy-start.3 = (bf16[2,128,64]{1,2,0:T(8,128)(2,1)S(1)}, bf16[2,128,64]{1,2,0:T(8,128)(2,1)}, u32[]{:S(2)}) copy-start(bf16[2,128,64]{1,2,0:T(8,128)(2,1)} %param.10) | copy-start | bytes 98308
  32.8 3.9 %copy-start.4 = (bf16[128,64]{0,1:T(8,128)(2,1)S(1)}, bf16[128,64]{0,1:T(8,128)(2,1)}, u32[]{:S(2)}) copy-start(bf16[128,64]{0,1:T(8,128)(2,1)} %param.11) | copy-start | bytes 49156
  48.2 6.5 %collective-permute-start.5 = (bf16[48,1024]{1,0:T(8,128)(2,1)S(1)}, bf16[48,1024]{1,0:T(8,128)(2,1)S(1)}, u32[]{:S(2)}, u32[]{:S(2)}) collective-permute-start(bf16[48,1024]{1,0:T(8,128)(2,1)S(1)} %get-tuple-element.42), channel_id=1, source_target_pairs={{0,1},{1,2},{2,3},{3,0},{4,5},{5,6},{6,7},{7,4},{8,9},{9,10},{10,1... | collective-permute-start | bytes 294920 | tf_op jit(solution)/shard_map/ppermute | solution.py:666
  49.8 7.0 %collective-permute-start.6 = (bf16[48,1024]{1,0:T(8,128)(2,1)S(1)}, bf16[48,1024]{1,0:T(8,128)(2,1)S(1)}, u32[]{:S(2)}, u32[]{:S(2)}) collective-permute-start(bf16[48,1024]{1,0:T(8,128)(2,1)S(1)} %get-tuple-element.43), channel_id=1, source_target_pairs={{0,2},{1,3},{2,0},{3,1},{4,6},{5,7},{6,4},{7,5},{8,10},{9,11},{10,... | collective-permute-start | bytes 294920 | tf_op jit(solution)/shard_map/ppermute | solution.py:666
  52.4 5.5 %collective-permute-start.7 = (bf16[48,1024]{1,0:T(8,128)(2,1)S(1)}, bf16[48,1024]{1,0:T(8,128)(2,1)S(1)}, u32[]{:S(2)}, u32[]{:S(2)}) collective-permute-start(bf16[48,1024]{1,0:T(8,128)(2,1)S(1)} %get-tuple-element.44), channel_id=1, source_target_pairs={{0,3},{1,0},{2,1},{3,2},{4,7},{5,4},{6,5},{7,6},{8,11},{9,8},{10,9... | collective-permute-start | bytes 294920 | tf_op jit(solution)/shard_map/ppermute | solution.py:666
where the time goes:
time: 78.2 us; the launch traced here: 77.9 us
  waiting for transfers between devices  21.9 us (28%)
  Pallas kernels  17.7 us (23%)
  blocking collectives  17.5 us (22%)
  starting transfers between devices  16.5 us (21%)
  other arithmetic  2.43 us (3%)
  local copies, waits for them, and re-layouts  1.03 us (1%)
  between operations  0.81 us (1%)
    ppermute x2, waiting for transfers between devices, hop(): lax.ppermute(x, 'seq', [(i, i + distance) for i in everyone if i + distan...  18.6 us
    all_gather x1, blocking collectives, shards(): gathered = lax.all_gather(out, 'seq')  17.5 us
    ppermute x2, starting transfers between devices, hop(): lax.ppermute(x, 'seq', [(i, i + distance) for i in everyone if i + distan...  8.33 us
    ppermute x3, starting transfers between devices, shards(): lax.ppermute(pieces[k], 'tensor', [(i, (i + k) % tensor) for i in range(t...  5.57 us
    pallas_call x1, Pallas kernels, shards(): pl.pallas_call(functools.partial(main_kernel, scale, 2.0 / (n * seq), flo...  5.54 us
    pallas_call x1, Pallas kernels, shards(): pl.pallas_call(student_kernel, out_shape=(wide, sds((width, n), F32), wid...  4.87 us
    pallas_call x1, Pallas kernels, shards(): pl.pallas_call(functools.partial(teacher_kernel, scale), out_shape=(sds((...  3.85 us
    ppermute x3, waiting for transfers between devices, shards(): lax.ppermute(pieces[k], 'tensor', [(i, (i + k) % tensor) for i in range(t...  3.28 us
  transfers between devices with their start and end apart: 8, of which 4 were waited for; matrix products, arithmetic and copies ran while one was open for 2% of the time, Pallas kernels for 13%

commit v1 on v0

--- a/solution.py
+++ b/solution.py
@@ -14,7 +14,8 @@
 TQ = 256
 TK = 1024
 TC = 256
-CH = 256
+CH = 512
+CHAINS = 4
 BF = jnp.bfloat16
 F32 = jnp.float32
 
@@ -137,6 +138,7 @@
     width = wink.shape[1]
     tile0 = begin_key // TK
     tiles = stop_key // TK
+    cut = jnp.minimum(begin_key - tile0 * TK, 1)
 
     @pl.when(begin_key < stop_key)
     def _():
@@ -155,7 +157,7 @@
             return carry
 
         lax.fori_loop(tile0, tiles, prepare, 0)
-        wq = max(TC, 2 * TC // heads)
+        wq = min(n, CHAINS * TC // heads)
         chains = [(h, c) for h in range(heads) for c in range(wq // TC)]
         factor = scale * LOG2E
 
@@ -206,16 +208,26 @@
                     stage(x, kt, x + 1, kt, masked)
                 stage(len(chains) - 1, kt, 0, jnp.minimum(kt + 1, tiles - 1), False)
 
-            smax_ref[0] = functools.reduce(
-                jnp.maximum, [scores(0, tile0, part, True) for part in range(TK // CH)]
-            )
-            sweep(tile0, True)
+            def prime(masked):
+                smax_ref[0] = functools.reduce(
+                    jnp.maximum, [scores(0, tile0, part, masked) for part in range(TK // CH)]
+                )
+
+            @pl.when(cut > 0)
+            def _():
+                prime(True)
+                sweep(tile0, True)
+
+            @pl.when(cut == 0)
+            def _():
+                prime(False)
+
 
             def step(kt, carry):
                 sweep(kt, False)
                 return carry
 
-            lax.fori_loop(tile0 + 1, tiles, step, 0)
+            lax.fori_loop(tile0 + cut, tiles, step, 0)
             i = lax.broadcasted_iota(jnp.int32, (1, wq), 1) + first
             live = i < lead_rows
             for x, (h, c) in enumerate(chains):
@@ -238,17 +250,15 @@
     n = start_ref.shape[1]
     heads = q_ref.shape[1] // width
     odd = lax.rem(lax.axis_index("seq"), 2)
-    begin(load(two_ref, 1, wink, winv, wcode, sem))
+    begin(load(two_ref, 0, wink, winv, wcode, sem))
 
     @pl.when(odd == 0)
     def _():
-        begin(load(swap_two_ref, 2, wink, winv, wcode, sem))
-        wcode[0] = jnp.zeros_like(wcode[0])
+        begin(load(swap_two_ref, 1, wink, winv, wcode, sem))
 
     @pl.when(odd == 1)
     def _():
-        begin(load(own_ref, 2, wink, winv, wcode, sem))
-        begin(load(swap_two_ref, 0, wink, winv, wcode, sem))
+        begin(load(own_ref, 1, wink, winv, wcode, sem))
 
     acc_ref[...] = acc_in[...]
     st2_ref[...] = stat_in[...]
@@ -256,12 +266,8 @@
     csum_ref[...] = jnp.zeros_like(csum_ref)
     lead_code = (doc_ref[0] + 1).astype(F32)
     lead_rows = jnp.sum((start_ref[...] == 0).astype(jnp.int32))
+    finish(load(two_ref, 0, wink, winv, wcode, sem))
     finish(load(two_ref, 1, wink, winv, wcode, sem))
-    finish(load(two_ref, 2, wink, winv, wcode, sem))
-
-    @pl.when(odd == 1)
-    def _():
-        finish(load(two_ref, 0, wink, winv, wcode, sem))
 
     stop_key = wink.shape[0]
     window_part(
@@ -290,19 +296,17 @@
     half = wk_ref.shape[0]
     odd = lax.rem(lax.axis_index("seq"), 2)
     begin(load(four_ref, 0, wink, winv, wcode, sem))
-    begin(load(two_ref, 1, neark, nearv, nearc, near_sem))
+    begin(load(two_ref, 0, neark, nearv, nearc, near_sem))
 
     @pl.when(odd == 0)
     def _():
         begin(load(swap_four_ref, 1, wink, winv, wcode, sem))
-        begin(load(swap_two_ref, 2, neark, nearv, nearc, near_sem))
-        nearc[0] = jnp.zeros_like(nearc[0])
+        begin(load(swap_two_ref, 1, neark, nearv, nearc, near_sem))
 
     @pl.when(odd == 1)
     def _():
-        begin(load(own_ref, 2, neark, nearv, nearc, near_sem))
-        begin(load(swap_two_ref, 0, neark, nearv, nearc, near_sem))
-        wcode[1] = jnp.zeros_like(wcode[1])
+        begin(load(swap_two_ref, 1, wink, winv, wcode, sem))
+        begin(load(own_ref, 1, neark, nearv, nearc, near_sem))
 
     gkf2_ref[...] = jnp.zeros_like(gkf2_ref)
     gwq_ref[...] = jnp.zeros_like(gwq_ref)
@@ -314,21 +318,13 @@
     st2_ref[...] = stat_in[...]
     lead_code = (doc_ref[0] + 1).astype(F32)
     lead_rows = jnp.sum((start_ref[...] == 0).astype(jnp.int32))
-    finish(load(four_ref, 0, wink, winv, wcode, sem))
-    finish(load(two_ref, 1, neark, nearv, nearc, near_sem))
-    finish(load(two_ref, 2, neark, nearv, nearc, near_sem))
-
-    @pl.when(odd == 0)
-    def _():
-        finish(load(four_ref, 1, wink, winv, wcode, sem))
-
-    @pl.when(odd == 1)
-    def _():
-        finish(load(two_ref, 0, neark, nearv, nearc, near_sem))
+    for slot in range(2):
+        finish(load(four_ref, slot, wink, winv, wcode, sem))
+        finish(load(two_ref, slot, neark, nearv, nearc, near_sem))
 
     near_stop = neark.shape[0]
     near_begin = near_stop - matching(nearc, lead_code)
-    far_stop = jnp.where(odd == 1, n, 2 * n)
+    far_stop = wink.shape[0]
     far_begin = far_stop - matching(wcode, lead_code)
     linked = near_begin < near_stop
     window_part(
@@ -574,8 +570,8 @@
     sds = jax.ShapeDtypeStruct
     cols = heads * n
     rows = width // tensor
-    near = REACH - 1
-    chains = max(heads, 2)
+    near = REACH // 2
+    chains = heads * min(n, CHAINS * TC // heads) // TC
     square = sds((width, width), F32)
     wide = sds((width, cols), F32)
     flat = sds((8, cols), F32)

time: 78.2 us -> 76.9 us (0.983)
  blocking collectives: 17.5 us -> 15.1 us
  waiting for transfers between devices: 21.9 us -> 23 us
    all_gather x1, blocking collectives: 17.5 us -> 15.1 us  [shards(): gathered = lax.all_gather(out, 'seq')]
    ppermute x3, waiting for transfers between devices: 3.28 us -> 4.39 us  [shards(): lax.ppermute(pieces[k], 'tensor', [(i, (i + k) % tensor) for i in range(t...]
where the time goes in v1:
time: 76.9 us; the launch traced here: 76.5 us
  waiting for transfers between devices  23 us (30%)
  Pallas kernels  17.7 us (23%)
  starting transfers between devices  16.5 us (21%)
  blocking collectives  15.1 us (20%)
  other arithmetic  2.43 us (3%)
  local copies, waits for them, and re-layouts  1.03 us (1%)
  between operations  0.81 us (1%)
    ppermute x2, waiting for transfers between devices, hop(): lax.ppermute(x, 'seq', [(i, i + distance) for i in everyone if i + distan...  18.6 us
    all_gather x1, blocking collectives, shards(): gathered = lax.all_gather(out, 'seq')  15.1 us
    ppermute x2, starting transfers between devices, hop(): lax.ppermute(x, 'seq', [(i, i + distance) for i in everyone if i + distan...  8.33 us
    ppermute x3, starting transfers between devices, shards(): lax.ppermute(pieces[k], 'tensor', [(i, (i + k) % tensor) for i in range(t...  5.57 us
    pallas_call x1, Pallas kernels, shards(): pl.pallas_call(functools.partial(main_kernel, scale, 2.0 / (n * seq), flo...  5.52 us
    pallas_call x1, Pallas kernels, shards(): pl.pallas_call(student_kernel, out_shape=(wide, sds((width, n), F32), wid...  4.87 us
    ppermute x3, waiting for transfers between devices, shards(): lax.ppermute(pieces[k], 'tensor', [(i, (i + k) % tensor) for i in range(t...  4.39 us
    pallas_call x1, Pallas kernels, shards(): pl.pallas_call(functools.partial(teacher_kernel, scale), out_shape=(sds((...  3.85 us
  transfers between devices with their start and end apart: 8, of which 4 were waited for; matrix products, arithmetic and copies ran while one was open for 2% of the time, Pallas kernels for 13%

profile of v1, /device:TPU:0, one launch (start us, length us, event | category | flops | bytes accessed | tf_op | source)
XLA Modules:
  0.0 76.5 jit_solution(1803787370399817903)
XLA Ops:
  0.6 0.0 copy-start.5
  0.6 0.8 fusion.2
  1.4 1.1 %fusion.1 = bf16[2064,128]{1,0:T(8,128)(2,1)S(1)} fusion(bf16[8,128]{1,0:T(8,128)(2,1)S(1)} %fusion.2, bf16[1024,128]{1,0:T(8,128)(2,1)} %v_ref.5, bf16[1024,128]{1,0:T(8,128)(2,1)} %k_ref.5), kind=kLoop, calls=%fused_computation.3 | loop fusion | flops 2113536 | bytes 1054720 | tf_op jit(solution)/shard_map/concatenate | solution.py:557
  2.5 4.9 %collective-permute-start.1 = (bf16[2064,128]{1,0:T(8,128)(2,1)S(1)}, bf16[2064,128]{1,0:T(8,128)(2,1)S(1)}, u32[]{:S(2)}, u32[]{:S(2)}) collective-permute-start(bf16[2064,128]{1,0:T(8,128)(2,1)S(1)} %fusion.1), channel_id=1, source_target_pairs={{0,8},{4,12},{8,16},{12,20},{16,24},{20,28},{1,9},{5,13},{9,17},{1... | collective-permute-start | bytes 1585160 | tf_op jit(solution)/shard_map/ppermute | solution.py:560
  7.4 3.4 %collective-permute-start.3 = (bf16[2064,128]{1,0:T(8,128)(2,1)S(1)}, bf16[2064,128]{1,0:T(8,128)(2,1)S(1)}, u32[]{:S(2)}, u32[]{:S(2)}) collective-permute-start(bf16[2064,128]{1,0:T(8,128)(2,1)S(1)} %fusion.1), channel_id=1, source_target_pairs={{0,16},{4,20},{8,24},{12,28},{1,17},{5,21},{9,25},{13,29},{2,18},{... | collective-permute-start | bytes 1585160 | tf_op jit(solution)/shard_map/ppermute | solution.py:560
  10.9 1.3 %collective-permute-start = (bf16[2064,128]{1,0:T(8,128)(2,1)S(1)}, bf16[2064,128]{1,0:T(8,128)(2,1)S(1)}, u32[]{:S(2)}, u32[]{:S(2)}) collective-permute-start(bf16[2064,128]{1,0:T(8,128)(2,1)S(1)} %fusion.1), channel_id=1, source_target_pairs={{0,4},{8,12},{16,20},{24,28},{1,5},{9,13},{17,21},{25,29},{2,6},{1... | collective-permute-start | bytes 1585160 | tf_op jit(solution)/shard_map/ppermute | solution.py:563
  12.2 6.5 %collective-permute-done.1.two_ref = bf16[2064,128]{1,0:T(8,128)(2,1)S(1)} collective-permute-done((bf16[2064,128]{1,0:T(8,128)(2,1)S(1)}, bf16[2064,128]{1,0:T(8,128)(2,1)S(1)}, u32[]{:S(2)}, u32[]{:S(2)}) %collective-permute-start.1) | collective-permute-done | bytes 528416 | tf_op jit(solution)/shard_map/ppermute | solution.py:560
  18.7 0.0 collective-permute-start.2
  18.7 0.0 copy-done.5
  18.7 0.1 copy.12
  18.8 12.2 %collective-permute-done.3.four_ref = bf16[2064,128]{1,0:T(8,128)(2,1)S(1)} collective-permute-done((bf16[2064,128]{1,0:T(8,128)(2,1)S(1)}, bf16[2064,128]{1,0:T(8,128)(2,1)S(1)}, u32[]{:S(2)}, u32[]{:S(2)}) %collective-permute-start.3) | collective-permute-done | bytes 528416 | tf_op jit(solution)/shard_map/ppermute | solution.py:560
  30.9 1.3 %collective-permute-start.4 = (bf16[2064,128]{1,0:T(8,128)(2,1)S(1)}, bf16[2064,128]{1,0:T(8,128)(2,1)S(1)}, u32[]{:S(2)}, u32[]{:S(2)}) collective-permute-start(bf16[2064,128]{1,0:T(8,128)(2,1)S(1)} %collective-permute-done.3.four_ref), channel_id=1, source_target_pairs={{4,0},{12,8},{20,16},{28,24},{5,1},{13,9},{21,17},{29,25},{6,2},{1... | collective-permute-start | bytes 1585160 | tf_op jit(solution)/shard_map/ppermute | solution.py:621
  32.2 0.6 convert_reduce_fusion.edge_ref
  32.8 0.0 copy-start.3
  32.8 0.0 copy-start.4
  32.8 3.9 %shard_map.93 = (bf16[128,1024]{1,0:T(8,128)(2,1)S(1)}, f32[128,2048]{1,0:T(8,128)S(1)}, f32[8,2048]{1,0:T(8,128)S(1)}) custom-call(bf16[1024,256]{1,0:T(8,128)(2,1)S(1)} %bitcast.14, bf16[1024,128]{1,0:T(8,128)(2,1)S(1)} %copy-done.1, bf16[1024,128]{1,0:T(8,128)(2,1)S(1)} %copy-done, s32[1,1024]{1,0:T(1,128)S(1)} %bitcast.18), custom_call_target="tpu_custom_call" | custom-call | flops 1073741824 | bytes 4194304 | tf_op jit(solution)/shard_map/pallas_call | solution.py:584
  36.7 4.9 %shard_map.94 = (f32[128,2048]{1,0:T(8,128)S(1)}, f32[128,1024]{1,0:T(8,128)S(1)}, f32[128,2048]{1,0:T(8,128)S(1)}, f32[8,2048]{1,0:T(8,128)S(1)}) custom-call(bf16[1024,256]{1,0:T(8,128)(2,1)S(1)} %bitcast.15, bf16[1024,128]{1,0:T(8,128)(2,1)S(1)} %copy-done.1, bf16[128,1024]{1,0:T(8,128)(2,1)S(1)} %get-tuple-element.27.vt_ref, s32[1,1024]{1,0:T(1,128)S(1)} %bitcast.19, ...), custom_call_target="tpu_custom_call" | custom-call | flops 1073741824 | bytes 4194304 | tf_op jit(solution)/shard_map/pallas_call | solution.py:593
  41.6 0.0 collective-permute-done.own_ref
  41.6 0.0 collective-permute-done.2.swap_two_ref
  41.6 1.0 %shard_map.95 = (f32[128,2048]{1,0:T(8,128)S(1)}, f32[8,2048]{1,0:T(8,128)S(1)}, f32[128,2048]{1,0:T(8,128)S(1)}, f32[128,128]{1,0:T(8,128)S(1)}, f32[128,128]{1,0:T(8,128)S(1)}) custom-call(s32[1024]{0:T(1024)S(1)} %copy-done.2, bf16[1024,256]{1,0:T(8,128)(2,1)S(1)} %bitcast.16, s32[1,1024]{1,0:T(1,128)S(1)} %bitcast.20, bf16[64,128]{1,0:T(8,128)(2,1)S(1)} %bitcast.24, ...), custom_call_target="tpu_custom_call" | custom-call | flops 2147483648 | bytes 4194304 | tf_op jit(solution)/shard_map/pallas_call | solution.py:604
  42.6 0.0 collective-permute-done.4.swap_four_ref
  42.6 5.5 %shard_map.96 = (bf16[1024,256]{1,0:T(8,128)(2,1)S(1)}, bf16[128,128]{1,0:T(8,128)(2,1)S(1)}, bf16[48,1024]{1,0:T(8,128)(2,1)S(1)}, bf16[48,1024]{1,0:T(8,128)(2...) custom-call(s32[1024]{0:T(1024)S(1)} %copy-done.2, bf16[1024,256]{1,0:T(8,128)(2,1)S(1)} %bitcast.17, ...), custom_call_target="tpu_custom_call" | custom-call | flops 4294967296 | bytes 8388608 | tf_op jit(solution)/shard_map/pallas_call | solution.py:622
  48.2 1.6 %collective-permute-start.5 = (bf16[48,1024]{1,0:T(8,128)(2,1)S(1)}, bf16[48,1024]{1,0:T(8,128)(2,1)S(1)}, u32[]{:S(2)}, u32[]{:S(2)}) collective-permute-start(bf16[48,1024]{1,0:T(8,128)(2,1)S(1)} %get-tuple-element.42), channel_id=1, source_target_pairs={{0,1},{1,2},{2,3},{3,0},{4,5},{5,6},{6,7},{7,4},{8,9},{9,10},{10,1... | collective-permute-start | bytes 294920 | tf_op jit(solution)/shard_map/ppermute | solution.py:662
  49.8 2.6 %collective-permute-start.6 = (bf16[48,1024]{1,0:T(8,128)(2,1)S(1)}, bf16[48,1024]{1,0:T(8,128)(2,1)S(1)}, u32[]{:S(2)}, u32[]{:S(2)}) collective-permute-start(bf16[48,1024]{1,0:T(8,128)(2,1)S(1)} %get-tuple-element.43), channel_id=1, source_target_pairs={{0,2},{1,3},{2,0},{3,1},{4,6},{5,7},{6,4},{7,5},{8,10},{9,11},{10,... | collective-permute-start | bytes 294920 | tf_op jit(solution)/shard_map/ppermute | solution.py:662
  52.4 1.4 %collective-permute-start.7 = (bf16[48,1024]{1,0:T(8,128)(2,1)S(1)}, bf16[48,1024]{1,0:T(8,128)(2,1)S(1)}, u32[]{:S(2)}, u32[]{:S(2)}) collective-permute-start(bf16[48,1024]{1,0:T(8,128)(2,1)S(1)} %get-tuple-element.44), channel_id=1, source_target_pairs={{0,3},{1,0},{2,1},{3,2},{4,7},{5,4},{6,5},{7,6},{8,11},{9,8},{10,9... | collective-permute-start | bytes 294920 | tf_op jit(solution)/shard_map/ppermute | solution.py:662
  53.7 0.9 %reshape.25 = bf16[1024,2,128]{2,1,0:T(2,128)(2,1)} reshape(bf16[1024,256]{1,0:T(8,128)(2,1)S(1)} %get-tuple-element.39) | data formatting | bytes 1048576 | tf_op jit(solution)/shard_map/reshape | solution.py:687
  54.7 0.0 collective-permute-done.5.refs_1_
  54.7 2.6 %collective-permute-done.6.refs_2_ = bf16[48,1024]{1,0:T(8,128)(2,1)S(1)} collective-permute-done((bf16[48,1024]{1,0:T(8,128)(2,1)S(1)}, bf16[48,1024]{1,0:T(8,128)(2,1)S(1)}, u32[]{:S(2)}, u32[]{:S(2)}) %collective-permute-start.6) | collective-permute-done | bytes 98336 | tf_op jit(solution)/shard_map/ppermute | solution.py:662
  57.3 1.8 %collective-permute-done.7.refs_3_ = bf16[48,1024]{1,0:T(8,128)(2,1)S(1)} collective-permute-done((bf16[48,1024]{1,0:T(8,128)(2,1)S(1)}, bf16[48,1024]{1,0:T(8,128)(2,1)S(1)}, u32[]{:S(2)}, u32[]{:S(2)}) %collective-permute-start.7) | collective-permute-done | bytes 98336 | tf_op jit(solution)/shard_map/ppermute | solution.py:662
  59.0 0.7 shard_map.97
  59.7 15.1 %all-gather = bf16[2432,128]{1,0:T(8,128)(2,1)S(1)} all-gather(bf16[304,128]{1,0:T(8,128)(2,1)S(1)} %get-tuple-element.45), channel_id=2, replica_groups=mesh['seq'=8,'tensor'=4] {'seq'}, dimensions={0}, use_global_device_ids=true | all-gather | bytes 700416 | tf_op jit(solution)/shard_map/all_gather | solution.py:673
  74.8 1.7 %shard_map.98 = (f32[32,1024]{1,0:T(8,128)}, f32[2,64,128]{2,1,0:T(8,128)}, f32[64,128]{1,0:T(8,128)}) custom-call(s32[1024]{0:T(1024)S(1)} %copy-done.2, s32[1024]{0:T(1024)S(1)} %convert_reduce_fusion.edge_ref, bf16[8,304,128]{2,1,0:T(8,128)(2,1)S(1)} %bitcast.13, f32[32,1024]{1,0:T(8,128)S(1)} %get-tuple-element.46.sum_ref, bf16[1024,128]{1,0:T(8,128)(2,1)S(1)} %copy-done), custom_call_target="tpu_custom_call" | custom-call | flops 67108864 | bytes 2097152 | tf_op jit(solution)/shard_map/pallas_call | solution.py:674
  (8 shorter events, 0.0 us)
Async XLA Ops:
  0.6 18.0 %copy-start.5 = (bf16[1024,2,128]{2,1,0:T(2,128)(2,1)S(1)}, bf16[1024,2,128]{2,1,0:T(2,128)(2,1)}, u32[]{:S(2)}) copy-start(bf16[1024,2,128]{2,1,0:T(2,128)(2,1)} %param.6) | copy-start | bytes 1572868
  1.4 30.8 %copy-start.2 = (s32[1024]{0:T(1024)S(1)}, s32[1024]{0:T(1024)}, u32[]{:S(2)}) copy-start(s32[1024]{0:T(1024)} %doc_ref.7) | copy-start | bytes 12292
  1.4 31.4 %copy-start = (bf16[1024,128]{1,0:T(8,128)(2,1)S(1)}, bf16[1024,128]{1,0:T(8,128)(2,1)}, u32[]{:S(2)}) copy-start(bf16[1024,128]{1,0:T(8,128)(2,1)} %v_ref.5) | copy-start | bytes 786436
  1.4 31.4 %copy-start.1 = (bf16[1024,128]{1,0:T(8,128)(2,1)S(1)}, bf16[1024,128]{1,0:T(8,128)(2,1)}, u32[]{:S(2)}) copy-start(bf16[1024,128]{1,0:T(8,128)(2,1)} %k_ref.5) | copy-start | bytes 786436
  2.5 16.1 %collective-permute-start.1 = (bf16[2064,128]{1,0:T(8,128)(2,1)S(1)}, bf16[2064,128]{1,0:T(8,128)(2,1)S(1)}, u32[]{:S(2)}, u32[]{:S(2)}) collective-permute-start(bf16[2064,128]{1,0:T(8,128)(2,1)S(1)} %fusion.1), channel_id=1, source_target_pairs={{0,8},{4,12},{8,16},{12,20},{16,24},{20,28},{1,9},{5,13},{9,17},{1... | collective-permute-start | bytes 1585160 | tf_op jit(solution)/shard_map/ppermute | solution.py:560
  7.4 23.5 %collective-permute-start.3 = (bf16[2064,128]{1,0:T(8,128)(2,1)S(1)}, bf16[2064,128]{1,0:T(8,128)(2,1)S(1)}, u32[]{:S(2)}, u32[]{:S(2)}) collective-permute-start(bf16[2064,128]{1,0:T(8,128)(2,1)S(1)} %fusion.1), channel_id=1, source_target_pairs={{0,16},{4,20},{8,24},{12,28},{1,17},{5,21},{9,25},{13,29},{2,18},{... | collective-permute-start | bytes 1585160 | tf_op jit(solution)/shard_map/ppermute | solution.py:560
  10.9 30.7 %collective-permute-start = (bf16[2064,128]{1,0:T(8,128)(2,1)S(1)}, bf16[2064,128]{1,0:T(8,128)(2,1)S(1)}, u32[]{:S(2)}, u32[]{:S(2)}) collective-permute-start(bf16[2064,128]{1,0:T(8,128)(2,1)S(1)} %fusion.1), channel_id=1, source_target_pairs={{0,4},{8,12},{16,20},{24,28},{1,5},{9,13},{17,21},{25,29},{2,6},{1... | collective-permute-start | bytes 1585160 | tf_op jit(solution)/shard_map/ppermute | solution.py:563
  18.7 22.9 %collective-permute-start.2 = (bf16[2064,128]{1,0:T(8,128)(2,1)S(1)}, bf16[2064,128]{1,0:T(8,128)(2,1)S(1)}, u32[]{:S(2)}, u32[]{:S(2)}) collective-permute-start(bf16[2064,128]{1,0:T(8,128)(2,1)S(1)} %collective-permute-done.1.two_ref), channel_id=1, source_target_pairs={{0,4},{4,0},{8,12},{12,8},{16,20},{20,16},{24,28},{28,24},{1,5},{5... | collective-permute-start | bytes 1585160 | tf_op jit(solution)/shard_map/ppermute | solution.py:603
  30.9 11.7 %collective-permute-start.4 = (bf16[2064,128]{1,0:T(8,128)(2,1)S(1)}, bf16[2064,128]{1,0:T(8,128)(2,1)S(1)}, u32[]{:S(2)}, u32[]{:S(2)}) collective-permute-start(bf16[2064,128]{1,0:T(8,128)(2,1)S(1)} %collective-permute-done.3.four_ref), channel_id=1, source_target_pairs={{4,0},{12,8},{20,16},{28,24},{5,1},{13,9},{21,17},{29,25},{6,2},{1... | collective-permute-start | bytes 1585160 | tf_op jit(solution)/shard_map/ppermute | solution.py:621
  32.8 3.9 %copy-start.3 = (bf16[2,128,64]{1,2,0:T(8,128)(2,1)S(1)}, bf16[2,128,64]{1,2,0:T(8,128)(2,1)}, u32[]{:S(2)}) copy-start(bf16[2,128,64]{1,2,0:T(8,128)(2,1)} %param.10) | copy-start | bytes 98308
  32.8 3.9 %copy-start.4 = (bf16[128,64]{0,1:T(8,128)(2,1)S(1)}, bf16[128,64]{0,1:T(8,128)(2,1)}, u32[]{:S(2)}) copy-start(bf16[128,64]{0,1:T(8,128)(2,1)} %param.11) | copy-start | bytes 49156
  48.2 6.5 %collective-permute-start.5 = (bf16[48,1024]{1,0:T(8,128)(2,1)S(1)}, bf16[48,1024]{1,0:T(8,128)(2,1)S(1)}, u32[]{:S(2)}, u32[]{:S(2)}) collective-permute-start(bf16[48,1024]{1,0:T(8,128)(2,1)S(1)} %get-tuple-element.42), channel_id=1, source_target_pairs={{0,1},{1,2},{2,3},{3,0},{4,5},{5,6},{6,7},{7,4},{8,9},{9,10},{10,1... | collective-permute-start | bytes 294920 | tf_op jit(solution)/shard_map/ppermute | solution.py:662
  49.8 7.5 %collective-permute-start.6 = (bf16[48,1024]{1,0:T(8,128)(2,1)S(1)}, bf16[48,1024]{1,0:T(8,128)(2,1)S(1)}, u32[]{:S(2)}, u32[]{:S(2)}) collective-permute-start(bf16[48,1024]{1,0:T(8,128)(2,1)S(1)} %get-tuple-element.43), channel_id=1, source_target_pairs={{0,2},{1,3},{2,0},{3,1},{4,6},{5,7},{6,4},{7,5},{8,10},{9,11},{10,... | collective-permute-start | bytes 294920 | tf_op jit(solution)/shard_map/ppermute | solution.py:662
  52.4 6.7 %collective-permute-start.7 = (bf16[48,1024]{1,0:T(8,128)(2,1)S(1)}, bf16[48,1024]{1,0:T(8,128)(2,1)S(1)}, u32[]{:S(2)}, u32[]{:S(2)}) collective-permute-start(bf16[48,1024]{1,0:T(8,128)(2,1)S(1)} %get-tuple-element.44), channel_id=1, source_target_pairs={{0,3},{1,0},{2,1},{3,2},{4,7},{5,4},{6,5},{7,6},{8,11},{9,8},{10,9... | collective-permute-start | bytes 294920 | tf_op jit(solution)/shard_map/ppermute | solution.py:662

commit v2 on v1

--- a/solution.py
+++ b/solution.py
@@ -133,7 +133,7 @@
 def window_part(
     scale, n, heads, begin_key, stop_key, lead_rows,
     q_ref, wk_ref, wink, winv, wkf, wvt, statet_ref, csum_ref,
-    acc_ref, st2_ref, run_ref, racc_ref, sbuf_ref, smax_ref,
+    acc_ref, st2_ref, run_ref, racc_ref, sbuf_ref, smax_ref, bias_ref,
 ):
     width = wink.shape[1]
     tile0 = begin_key // TK
@@ -157,6 +157,8 @@
             return carry
 
         lax.fori_loop(tile0, tiles, prepare, 0)
+        key = lax.broadcasted_iota(jnp.int32, bias_ref.shape, 0) + tile0 * TK
+        bias_ref[...] = jnp.where(key >= begin_key, 0.0, NEG)
         wq = min(n, CHAINS * TC // heads)
         chains = [(h, c) for h in range(heads) for c in range(wq // TC)]
         factor = scale * LOG2E
@@ -179,8 +181,8 @@
                 row = pl.multiple_of(kt * TK + part * CH, CH)
                 s = mm(wink[pl.ds(row, CH)], q, NT)
                 if masked:
-                    j = lax.broadcasted_iota(jnp.int32, (CH, 1), 0) + row
-                    s = jnp.where(j >= begin_key, s, NEG)
+                    bias = bias_ref[part * CH : (part + 1) * CH]
+                    s = s + jnp.concatenate([bias] * (TC // 128), axis=1)
                 sbuf_ref[x, part * CH : (part + 1) * CH] = s
                 return jnp.max(s.reshape(CH // 8, 8, TC), axis=0)
 
@@ -244,7 +246,7 @@
     scale,
     doc_ref, q_ref, start_ref, wk_ref, acc_in, stat_in, own_ref, two_ref, swap_two_ref,
     acc_ref, st2_ref, wkf, statet_ref, csum_ref,
-    wink, winv, wcode, wvt, run_ref, racc_ref, sbuf_ref, smax_ref, sem,
+    wink, winv, wcode, wvt, run_ref, racc_ref, sbuf_ref, smax_ref, bias_ref, sem,
 ):
     width = wk_ref.shape[1]
     n = start_ref.shape[1]
@@ -273,7 +275,7 @@
     window_part(
         scale, n, heads, stop_key - matching(wcode, lead_code), stop_key, lead_rows,
         q_ref, wk_ref, wink, winv, wkf, wvt, statet_ref, csum_ref,
-        acc_ref, st2_ref, run_ref, racc_ref, sbuf_ref, smax_ref,
+        acc_ref, st2_ref, run_ref, racc_ref, sbuf_ref, smax_ref, bias_ref,
     )
 
 
@@ -289,7 +291,7 @@
         neark, nearv, nearc, wink, winv, wcode, wkf, wvt,
         gwq_ref, gwk_ref, adj_ref, adjs_ref, gkf_ref, gkf2_ref,
         state_ref, statet_ref, csum_ref, acc_ref, st2_ref, run_ref, racc_ref, sbuf_ref, smax_ref,
-        near_sem, sem,
+        bias_ref, near_sem, sem,
     ) = rest[tensor_size:]
     n, width = k_ref.shape
     heads = q_ref.shape[1] // width
@@ -320,7 +322,7 @@
     lead_rows = jnp.sum((start_ref[...] == 0).astype(jnp.int32))
     for slot in range(2):
         finish(load(four_ref, slot, wink, winv, wcode, sem))
-        finish(load(two_ref, slot, neark, nearv, nearc, near_sem))
+        finish(load(two_ref, slot, neark, nearv, nearc, near_sem)[2:])
 
     near_stop = neark.shape[0]
     near_begin = near_stop - matching(nearc, lead_code)
@@ -330,7 +332,7 @@
     window_part(
         scale, n, heads, far_begin, far_stop, lead_rows,
         q_ref, wk_ref, wink, winv, wkf, wvt, statet_ref, csum_ref,
-        acc_ref, st2_ref, run_ref, racc_ref, sbuf_ref, smax_ref,
+        acc_ref, st2_ref, run_ref, racc_ref, sbuf_ref, smax_ref, bias_ref,
     )
     state_ref[...] = statet_ref[...].T
     csum_ref[...] = jnp.broadcast_to(
@@ -378,18 +380,18 @@
         g_r = jnp.concatenate([(gn * r).astype(BF), (gd_rows * r).astype(BF)], axis=0)
         held[t] = (first, limit, h, qf_b, qf_r, g, g_r)
 
-    def first_product(t):
-        held[t] += (mm(v_aug[: held[t][1]], held[t][5]),)
-
     def second_product(t):
-        first, limit, h, qf_b, qf_r, g, g_r, raw = held[t]
+        first, limit, h, qf_b, qf_r, g, g_r = held[t]
         start = start_ref[:, first:limit]
-        j = lax.broadcasted_iota(jnp.int32, (TQ, TQ), 0) + first
         i = lax.broadcasted_iota(jnp.int32, (1, TQ), 1) + first
-        gp = jnp.where((j <= i) & (j >= start), raw[first:], 0.0).astype(BF)
-        if first:
-            j = lax.broadcasted_iota(jnp.int32, (first, TQ), 0)
-            gp = jnp.concatenate([jnp.where(j >= start, raw[:first], 0.0).astype(BF), gp], axis=0)
+        parts = []
+        for at in range(0, limit, TQ):
+            j = lax.broadcasted_iota(jnp.int32, (TQ, TQ), 0) + at
+            ok = j >= start
+            if at == first:
+                ok = ok & (j <= i)
+            parts.append(jnp.where(ok, mm(v_aug[at : at + TQ], g), 0.0).astype(BF))
+        gp = jnp.concatenate(parts, axis=0)
         gkf2_ref[:limit] += mm(gp, qf_b, NT)
         adj_ref[...] += mm(qf_r, g, NT)
         held[t] = (first, limit, h, mm(jnp.concatenate([kft_b[:, :limit], state_aug], axis=1), jnp.concatenate([gp, g_r], axis=0)))
@@ -402,11 +404,9 @@
 
     count = len(steps)
     before(0)
-    first_product(0)
     for t in range(count):
         if t + 1 < count:
             before(t + 1)
-            first_product(t + 1)
         second_product(t)
         if t:
             after(t - 1)
@@ -431,6 +431,8 @@
 
         lax.fori_loop(begin_key // TK, stop_key // TK, back, 0)
 
+    for slot in range(2):
+        finish(load(two_ref, slot, neark, nearv, nearc, near_sem)[:2])
     back_over(near_begin, near_stop, neark, nearv, near_kf)
     back_over(far_begin, far_stop, wink, winv, wkf)
 
@@ -552,7 +554,7 @@
     everyone = range(seq)
     assert n // width <= 16 and n // width * 16 == width
 
-    codes = (doc_ids + 1).astype(BF).reshape(n // width, width)
+    codes = (doc_ids.reshape(n // width, width) + 1).astype(BF)
     codes = jnp.pad(codes, ((0, 16 - n // width), (0, 0)))
     pack = jnp.concatenate([keys, values, codes], axis=0)
 
@@ -580,6 +582,7 @@
         pltpu.VMEM((chains, width, TC), F32),
         pltpu.VMEM((chains, TK, TC), F32),
         pltpu.VMEM((chains, 8, TC), F32),
+        pltpu.VMEM((TK, 128), F32),
     ]
     vt, acc, stat = pl.pallas_call(
         functools.partial(teacher_kernel, scale),

time: 76.9 us -> 76.6 us (level)
  no operation moved by 1% of the time
where the time goes in v2:
time: 76.6 us; the launch traced here: 76.2 us
  waiting for transfers between devices  23 us (30%)
  Pallas kernels  17.3 us (23%)
  starting transfers between devices  16.5 us (22%)
  blocking collectives  15.1 us (20%)
  other arithmetic  2.43 us (3%)
  local copies, waits for them, and re-layouts  1.03 us (1%)
  between operations  0.81 us (1%)
    ppermute x2, waiting for transfers between devices, hop(): lax.ppermute(x, 'seq', [(i, i + distance) for i in everyone if i + distan...  18.6 us
    all_gather x1, blocking collectives, shards(): gathered = lax.all_gather(out, 'seq')  15.1 us
    ppermute x2, starting transfers between devices, hop(): lax.ppermute(x, 'seq', [(i, i + distance) for i in everyone if i + distan...  8.33 us
    ppermute x3, starting transfers between devices, shards(): lax.ppermute(pieces[k], 'tensor', [(i, (i + k) % tensor) for i in range(t...  5.57 us
    pallas_call x1, Pallas kernels, shards(): pl.pallas_call(functools.partial(main_kernel, scale, 2.0 / (n * seq), flo...  5.19 us
    pallas_call x1, Pallas kernels, shards(): pl.pallas_call(student_kernel, out_shape=(wide, sds((width, n), F32), wid...  4.87 us
    ppermute x3, waiting for transfers between devices, shards(): lax.ppermute(pieces[k], 'tensor', [(i, (i + k) % tensor) for i in range(t...  4.36 us
    pallas_call x1, Pallas kernels, shards(): pl.pallas_call(functools.partial(teacher_kernel, scale), out_shape=(sds((...  3.85 us
  transfers between devices with their start and end apart: 8, of which 4 were waited for; matrix products, arithmetic and copies ran while one was open for 2% of the time, Pallas kernels for 13%

profile of v2, /device:TPU:0, one launch (start us, length us, event | category | flops | bytes accessed | tf_op | source)
XLA Modules:
  0.0 76.2 jit_solution(13011455876621165711)
XLA Ops:
  0.6 0.0 copy-start.5
  0.6 0.8 fusion.2
  1.4 1.1 %fusion.1 = bf16[2064,128]{1,0:T(8,128)(2,1)S(1)} fusion(bf16[8,128]{1,0:T(8,128)(2,1)S(1)} %fusion.2, bf16[1024,128]{1,0:T(8,128)(2,1)} %v_ref.5, bf16[1024,128]{1,0:T(8,128)(2,1)} %k_ref.5), kind=kLoop, calls=%fused_computation.3 | loop fusion | flops 2113536 | bytes 1054720 | tf_op jit(solution)/shard_map/concatenate | solution.py:559
  2.5 4.9 %collective-permute-start.1 = (bf16[2064,128]{1,0:T(8,128)(2,1)S(1)}, bf16[2064,128]{1,0:T(8,128)(2,1)S(1)}, u32[]{:S(2)}, u32[]{:S(2)}) collective-permute-start(bf16[2064,128]{1,0:T(8,128)(2,1)S(1)} %fusion.1), channel_id=1, source_target_pairs={{0,8},{4,12},{8,16},{12,20},{16,24},{20,28},{1,9},{5,13},{9,17},{1... | collective-permute-start | bytes 1585160 | tf_op jit(solution)/shard_map/ppermute | solution.py:562
  7.4 3.4 %collective-permute-start.3 = (bf16[2064,128]{1,0:T(8,128)(2,1)S(1)}, bf16[2064,128]{1,0:T(8,128)(2,1)S(1)}, u32[]{:S(2)}, u32[]{:S(2)}) collective-permute-start(bf16[2064,128]{1,0:T(8,128)(2,1)S(1)} %fusion.1), channel_id=1, source_target_pairs={{0,16},{4,20},{8,24},{12,28},{1,17},{5,21},{9,25},{13,29},{2,18},{... | collective-permute-start | bytes 1585160 | tf_op jit(solution)/shard_map/ppermute | solution.py:562
  10.9 1.3 %collective-permute-start = (bf16[2064,128]{1,0:T(8,128)(2,1)S(1)}, bf16[2064,128]{1,0:T(8,128)(2,1)S(1)}, u32[]{:S(2)}, u32[]{:S(2)}) collective-permute-start(bf16[2064,128]{1,0:T(8,128)(2,1)S(1)} %fusion.1), channel_id=1, source_target_pairs={{0,4},{8,12},{16,20},{24,28},{1,5},{9,13},{17,21},{25,29},{2,6},{1... | collective-permute-start | bytes 1585160 | tf_op jit(solution)/shard_map/ppermute | solution.py:565
  12.2 6.5 %collective-permute-done.1.two_ref = bf16[2064,128]{1,0:T(8,128)(2,1)S(1)} collective-permute-done((bf16[2064,128]{1,0:T(8,128)(2,1)S(1)}, bf16[2064,128]{1,0:T(8,128)(2,1)S(1)}, u32[]{:S(2)}, u32[]{:S(2)}) %collective-permute-start.1) | collective-permute-done | bytes 528416 | tf_op jit(solution)/shard_map/ppermute | solution.py:562
  18.7 0.0 collective-permute-start.2
  18.7 0.0 copy-done.5
  18.7 0.1 copy.12
  18.8 12.2 %collective-permute-done.3.four_ref = bf16[2064,128]{1,0:T(8,128)(2,1)S(1)} collective-permute-done((bf16[2064,128]{1,0:T(8,128)(2,1)S(1)}, bf16[2064,128]{1,0:T(8,128)(2,1)S(1)}, u32[]{:S(2)}, u32[]{:S(2)}) %collective-permute-start.3) | collective-permute-done | bytes 528416 | tf_op jit(solution)/shard_map/ppermute | solution.py:562
  30.9 1.3 %collective-permute-start.4 = (bf16[2064,128]{1,0:T(8,128)(2,1)S(1)}, bf16[2064,128]{1,0:T(8,128)(2,1)S(1)}, u32[]{:S(2)}, u32[]{:S(2)}) collective-permute-start(bf16[2064,128]{1,0:T(8,128)(2,1)S(1)} %collective-permute-done.3.four_ref), channel_id=1, source_target_pairs={{4,0},{12,8},{20,16},{28,24},{5,1},{13,9},{21,17},{29,25},{6,2},{1... | collective-permute-start | bytes 1585160 | tf_op jit(solution)/shard_map/ppermute | solution.py:624
  32.2 0.6 convert_reduce_fusion.edge_ref
  32.8 0.0 copy-start.3
  32.8 0.0 copy-start.4
  32.8 3.9 %shard_map.93 = (bf16[128,1024]{1,0:T(8,128)(2,1)S(1)}, f32[128,2048]{1,0:T(8,128)S(1)}, f32[8,2048]{1,0:T(8,128)S(1)}) custom-call(bf16[1024,256]{1,0:T(8,128)(2,1)S(1)} %bitcast.14, bf16[1024,128]{1,0:T(8,128)(2,1)S(1)} %copy-done.1, bf16[1024,128]{1,0:T(8,128)(2,1)S(1)} %copy-done, s32[1,1024]{1,0:T(1,128)S(1)} %bitcast.18), custom_call_target="tpu_custom_call" | custom-call | flops 1073741824 | bytes 4194304 | tf_op jit(solution)/shard_map/pallas_call | solution.py:587
  36.7 4.9 %shard_map.94 = (f32[128,2048]{1,0:T(8,128)S(1)}, f32[128,1024]{1,0:T(8,128)S(1)}, f32[128,2048]{1,0:T(8,128)S(1)}, f32[8,2048]{1,0:T(8,128)S(1)}) custom-call(bf16[1024,256]{1,0:T(8,128)(2,1)S(1)} %bitcast.15, bf16[1024,128]{1,0:T(8,128)(2,1)S(1)} %copy-done.1, bf16[128,1024]{1,0:T(8,128)(2,1)S(1)} %get-tuple-element.27.vt_ref, s32[1,1024]{1,0:T(1,128)S(1)} %bitcast.19, ...), custom_call_target="tpu_custom_call" | custom-call | flops 1073741824 | bytes 4194304 | tf_op jit(solution)/shard_map/pallas_call | solution.py:596
  41.6 0.0 collective-permute-done.own_ref
  41.6 0.0 collective-permute-done.2.swap_two_ref
  41.6 1.0 %shard_map.95 = (f32[128,2048]{1,0:T(8,128)S(1)}, f32[8,2048]{1,0:T(8,128)S(1)}, f32[128,2048]{1,0:T(8,128)S(1)}, f32[128,128]{1,0:T(8,128)S(1)}, f32[128,128]{1,0:T(8,128)S(1)}) custom-call(s32[1024]{0:T(1024)S(1)} %copy-done.2, bf16[1024,256]{1,0:T(8,128)(2,1)S(1)} %bitcast.16, s32[1,1024]{1,0:T(1,128)S(1)} %bitcast.20, bf16[64,128]{1,0:T(8,128)(2,1)S(1)} %bitcast.24, ...), custom_call_target="tpu_custom_call" | custom-call | flops 2147483648 | bytes 4194304 | tf_op jit(solution)/shard_map/pallas_call | solution.py:607
  42.6 0.0 collective-permute-done.4.swap_four_ref
  42.6 5.2 %shard_map.96 = (bf16[1024,256]{1,0:T(8,128)(2,1)S(1)}, bf16[128,128]{1,0:T(8,128)(2,1)S(1)}, bf16[48,1024]{1,0:T(8,128)(2,1)S(1)}, bf16[48,1024]{1,0:T(8,128)(2...) custom-call(s32[1024]{0:T(1024)S(1)} %copy-done.2, bf16[1024,256]{1,0:T(8,128)(2,1)S(1)} %bitcast.17, ...), custom_call_target="tpu_custom_call" | custom-call | flops 4294967296 | bytes 8388608 | tf_op jit(solution)/shard_map/pallas_call | solution.py:625
  47.8 1.6 %collective-permute-start.5 = (bf16[48,1024]{1,0:T(8,128)(2,1)S(1)}, bf16[48,1024]{1,0:T(8,128)(2,1)S(1)}, u32[]{:S(2)}, u32[]{:S(2)}) collective-permute-start(bf16[48,1024]{1,0:T(8,128)(2,1)S(1)} %get-tuple-element.42), channel_id=1, source_target_pairs={{0,1},{1,2},{2,3},{3,0},{4,5},{5,6},{6,7},{7,4},{8,9},{9,10},{10,1... | collective-permute-start | bytes 294920 | tf_op jit(solution)/shard_map/ppermute | solution.py:665
  49.5 2.6 %collective-permute-start.6 = (bf16[48,1024]{1,0:T(8,128)(2,1)S(1)}, bf16[48,1024]{1,0:T(8,128)(2,1)S(1)}, u32[]{:S(2)}, u32[]{:S(2)}) collective-permute-start(bf16[48,1024]{1,0:T(8,128)(2,1)S(1)} %get-tuple-element.43), channel_id=1, source_target_pairs={{0,2},{1,3},{2,0},{3,1},{4,6},{5,7},{6,4},{7,5},{8,10},{9,11},{10,... | collective-permute-start | bytes 294920 | tf_op jit(solution)/shard_map/ppermute | solution.py:665
  52.0 1.4 %collective-permute-start.7 = (bf16[48,1024]{1,0:T(8,128)(2,1)S(1)}, bf16[48,1024]{1,0:T(8,128)(2,1)S(1)}, u32[]{:S(2)}, u32[]{:S(2)}) collective-permute-start(bf16[48,1024]{1,0:T(8,128)(2,1)S(1)} %get-tuple-element.44), channel_id=1, source_target_pairs={{0,3},{1,0},{2,1},{3,2},{4,7},{5,4},{6,5},{7,6},{8,11},{9,8},{10,9... | collective-permute-start | bytes 294920 | tf_op jit(solution)/shard_map/ppermute | solution.py:665
  53.4 0.9 %reshape.25 = bf16[1024,2,128]{2,1,0:T(2,128)(2,1)} reshape(bf16[1024,256]{1,0:T(8,128)(2,1)S(1)} %get-tuple-element.39) | data formatting | bytes 1048576 | tf_op jit(solution)/shard_map/reshape | solution.py:690
  54.3 0.0 collective-permute-done.5.refs_1_
  54.3 2.5 %collective-permute-done.6.refs_2_ = bf16[48,1024]{1,0:T(8,128)(2,1)S(1)} collective-permute-done((bf16[48,1024]{1,0:T(8,128)(2,1)S(1)}, bf16[48,1024]{1,0:T(8,128)(2,1)S(1)}, u32[]{:S(2)}, u32[]{:S(2)}) %collective-permute-start.6) | collective-permute-done | bytes 98336 | tf_op jit(solution)/shard_map/ppermute | solution.py:665
  56.9 1.8 %collective-permute-done.7.refs_3_ = bf16[48,1024]{1,0:T(8,128)(2,1)S(1)} collective-permute-done((bf16[48,1024]{1,0:T(8,128)(2,1)S(1)}, bf16[48,1024]{1,0:T(8,128)(2,1)S(1)}, u32[]{:S(2)}, u32[]{:S(2)}) %collective-permute-start.7) | collective-permute-done | bytes 98336 | tf_op jit(solution)/shard_map/ppermute | solution.py:665
  58.7 0.7 shard_map.97
  59.3 15.1 %all-gather = bf16[2432,128]{1,0:T(8,128)(2,1)S(1)} all-gather(bf16[304,128]{1,0:T(8,128)(2,1)S(1)} %get-tuple-element.45), channel_id=2, replica_groups=mesh['seq'=8,'tensor'=4] {'seq'}, dimensions={0}, use_global_device_ids=true | all-gather | bytes 700416 | tf_op jit(solution)/shard_map/all_gather | solution.py:676
  74.4 1.7 %shard_map.98 = (f32[32,1024]{1,0:T(8,128)}, f32[2,64,128]{2,1,0:T(8,128)}, f32[64,128]{1,0:T(8,128)}) custom-call(s32[1024]{0:T(1024)S(1)} %copy-done.2, s32[1024]{0:T(1024)S(1)} %convert_reduce_fusion.edge_ref, bf16[8,304,128]{2,1,0:T(8,128)(2,1)S(1)} %bitcast.13, f32[32,1024]{1,0:T(8,128)S(1)} %get-tuple-element.46.sum_ref, bf16[1024,128]{1,0:T(8,128)(2,1)S(1)} %copy-done), custom_call_target="tpu_custom_call" | custom-call | flops 67108864 | bytes 2097152 | tf_op jit(solution)/shard_map/pallas_call | solution.py:677
  (8 shorter events, 0.0 us)
Async XLA Ops:
  0.6 18.0 %copy-start.5 = (bf16[1024,2,128]{2,1,0:T(2,128)(2,1)S(1)}, bf16[1024,2,128]{2,1,0:T(2,128)(2,1)}, u32[]{:S(2)}) copy-start(bf16[1024,2,128]{2,1,0:T(2,128)(2,1)} %param.6) | copy-start | bytes 1572868
  1.4 30.8 %copy-start.2 = (s32[1024]{0:T(1024)S(1)}, s32[1024]{0:T(1024)}, u32[]{:S(2)}) copy-start(s32[1024]{0:T(1024)} %doc_ref.7) | copy-start | bytes 12292
  1.4 31.4 %copy-start = (bf16[1024,128]{1,0:T(8,128)(2,1)S(1)}, bf16[1024,128]{1,0:T(8,128)(2,1)}, u32[]{:S(2)}) copy-start(bf16[1024,128]{1,0:T(8,128)(2,1)} %v_ref.5) | copy-start | bytes 786436
  1.4 31.4 %copy-start.1 = (bf16[1024,128]{1,0:T(8,128)(2,1)S(1)}, bf16[1024,128]{1,0:T(8,128)(2,1)}, u32[]{:S(2)}) copy-start(bf16[1024,128]{1,0:T(8,128)(2,1)} %k_ref.5) | copy-start | bytes 786436
  2.5 16.1 %collective-permute-start.1 = (bf16[2064,128]{1,0:T(8,128)(2,1)S(1)}, bf16[2064,128]{1,0:T(8,128)(2,1)S(1)}, u32[]{:S(2)}, u32[]{:S(2)}) collective-permute-start(bf16[2064,128]{1,0:T(8,128)(2,1)S(1)} %fusion.1), channel_id=1, source_target_pairs={{0,8},{4,12},{8,16},{12,20},{16,24},{20,28},{1,9},{5,13},{9,17},{1... | collective-permute-start | bytes 1585160 | tf_op jit(solution)/shard_map/ppermute | solution.py:562
  7.4 23.5 %collective-permute-start.3 = (bf16[2064,128]{1,0:T(8,128)(2,1)S(1)}, bf16[2064,128]{1,0:T(8,128)(2,1)S(1)}, u32[]{:S(2)}, u32[]{:S(2)}) collective-permute-start(bf16[2064,128]{1,0:T(8,128)(2,1)S(1)} %fusion.1), channel_id=1, source_target_pairs={{0,16},{4,20},{8,24},{12,28},{1,17},{5,21},{9,25},{13,29},{2,18},{... | collective-permute-start | bytes 1585160 | tf_op jit(solution)/shard_map/ppermute | solution.py:562
  10.9 30.7 %collective-permute-start = (bf16[2064,128]{1,0:T(8,128)(2,1)S(1)}, bf16[2064,128]{1,0:T(8,128)(2,1)S(1)}, u32[]{:S(2)}, u32[]{:S(2)}) collective-permute-start(bf16[2064,128]{1,0:T(8,128)(2,1)S(1)} %fusion.1), channel_id=1, source_target_pairs={{0,4},{8,12},{16,20},{24,28},{1,5},{9,13},{17,21},{25,29},{2,6},{1... | collective-permute-start | bytes 1585160 | tf_op jit(solution)/shard_map/ppermute | solution.py:565
  18.7 22.9 %collective-permute-start.2 = (bf16[2064,128]{1,0:T(8,128)(2,1)S(1)}, bf16[2064,128]{1,0:T(8,128)(2,1)S(1)}, u32[]{:S(2)}, u32[]{:S(2)}) collective-permute-start(bf16[2064,128]{1,0:T(8,128)(2,1)S(1)} %collective-permute-done.1.two_ref), channel_id=1, source_target_pairs={{0,4},{4,0},{8,12},{12,8},{16,20},{20,16},{24,28},{28,24},{1,5},{5... | collective-permute-start | bytes 1585160 | tf_op jit(solution)/shard_map/ppermute | solution.py:606
  30.9 11.7 %collective-permute-start.4 = (bf16[2064,128]{1,0:T(8,128)(2,1)S(1)}, bf16[2064,128]{1,0:T(8,128)(2,1)S(1)}, u32[]{:S(2)}, u32[]{:S(2)}) collective-permute-start(bf16[2064,128]{1,0:T(8,128)(2,1)S(1)} %collective-permute-done.3.four_ref), channel_id=1, source_target_pairs={{4,0},{12,8},{20,16},{28,24},{5,1},{13,9},{21,17},{29,25},{6,2},{1... | collective-permute-start | bytes 1585160 | tf_op jit(solution)/shard_map/ppermute | solution.py:624
  32.8 3.9 %copy-start.3 = (bf16[2,128,64]{1,2,0:T(8,128)(2,1)S(1)}, bf16[2,128,64]{1,2,0:T(8,128)(2,1)}, u32[]{:S(2)}) copy-start(bf16[2,128,64]{1,2,0:T(8,128)(2,1)} %param.10) | copy-start | bytes 98308
  32.8 3.9 %copy-start.4 = (bf16[128,64]{0,1:T(8,128)(2,1)S(1)}, bf16[128,64]{0,1:T(8,128)(2,1)}, u32[]{:S(2)}) copy-start(bf16[128,64]{0,1:T(8,128)(2,1)} %param.11) | copy-start | bytes 49156
  47.8 6.5 %collective-permute-start.5 = (bf16[48,1024]{1,0:T(8,128)(2,1)S(1)}, bf16[48,1024]{1,0:T(8,128)(2,1)S(1)}, u32[]{:S(2)}, u32[]{:S(2)}) collective-permute-start(bf16[48,1024]{1,0:T(8,128)(2,1)S(1)} %get-tuple-element.42), channel_id=1, source_target_pairs={{0,1},{1,2},{2,3},{3,0},{4,5},{5,6},{6,7},{7,4},{8,9},{9,10},{10,1... | collective-permute-start | bytes 294920 | tf_op jit(solution)/shard_map/ppermute | solution.py:665
  49.5 7.4 %collective-permute-start.6 = (bf16[48,1024]{1,0:T(8,128)(2,1)S(1)}, bf16[48,1024]{1,0:T(8,128)(2,1)S(1)}, u32[]{:S(2)}, u32[]{:S(2)}) collective-permute-start(bf16[48,1024]{1,0:T(8,128)(2,1)S(1)} %get-tuple-element.43), channel_id=1, source_target_pairs={{0,2},{1,3},{2,0},{3,1},{4,6},{5,7},{6,4},{7,5},{8,10},{9,11},{10,... | collective-permute-start | bytes 294920 | tf_op jit(solution)/shard_map/ppermute | solution.py:665
  52.0 6.6 %collective-permute-start.7 = (bf16[48,1024]{1,0:T(8,128)(2,1)S(1)}, bf16[48,1024]{1,0:T(8,128)(2,1)S(1)}, u32[]{:S(2)}, u32[]{:S(2)}) collective-permute-start(bf16[48,1024]{1,0:T(8,128)(2,1)S(1)} %get-tuple-element.44), channel_id=1, source_target_pairs={{0,3},{1,0},{2,1},{3,2},{4,7},{5,4},{6,5},{7,6},{8,11},{9,8},{10,9... | collective-permute-start | bytes 294920 | tf_op jit(solution)/shard_map/ppermute | solution.py:665

commit v3 on v2

--- a/solution.py
+++ b/solution.py
@@ -175,9 +175,9 @@
                 run_ref[x, 1:2] = st2_ref[1:2, col]
                 racc_ref[x] = acc_ref[:, col]
 
-            def scores(x, kt, part, masked):
+            def scores(x, base, kt, part, masked):
                 h, c = chains[x]
-                q = q_ref[pl.ds(first + c * TC, TC), h * width : (h + 1) * width]
+                q = q_ref[pl.ds(base + c * TC, TC), h * width : (h + 1) * width]
                 row = pl.multiple_of(kt * TK + part * CH, CH)
                 s = mm(wink[pl.ds(row, CH)], q, NT)
                 if masked:
@@ -186,12 +186,12 @@
                 sbuf_ref[x, part * CH : (part + 1) * CH] = s
                 return jnp.max(s.reshape(CH // 8, 8, TC), axis=0)
 
-            def stage(cur, kt, nxt, kt_nxt, masked):
+            def stage(cur, kt, nxt, base, kt_nxt, masked):
                 old = run_ref[cur, 0:1]
                 new = jnp.maximum(old, jnp.max(smax_ref[cur], axis=0, keepdims=True))
                 tops, sums, parts = [], [], []
                 for part in range(TK // CH):
-                    tops.append(scores(nxt, kt_nxt, part, masked))
+                    tops.append(scores(nxt, base, kt_nxt, part, masked))
                     w = jnp.exp2((sbuf_ref[cur, part * CH : (part + 1) * CH] - new) * factor)
                     sums.append(jnp.sum(w.reshape(CH // 8, 8, TC), axis=0))
                     parts.append(w.astype(BF))
@@ -207,12 +207,16 @@
 
             def sweep(kt, masked):
                 for x in range(len(chains) - 1):
-                    stage(x, kt, x + 1, kt, masked)
-                stage(len(chains) - 1, kt, 0, jnp.minimum(kt + 1, tiles - 1), False)
+                    stage(x, kt, x + 1, first, kt, masked)
+                turn = (kt + 1 == tiles) & (cut == 0)
+                after_kt = jnp.where(turn, tile0, jnp.minimum(kt + 1, tiles - 1))
+                after_first = jnp.where(turn, jnp.minimum(first + wq, n - wq), first)
+                base = pl.multiple_of(after_first, wq)
+                stage(len(chains) - 1, kt, 0, base, after_kt, False)
 
             def prime(masked):
                 smax_ref[0] = functools.reduce(
-                    jnp.maximum, [scores(0, tile0, part, masked) for part in range(TK // CH)]
+                    jnp.maximum, [scores(0, first, tile0, part, masked) for part in range(TK // CH)]
                 )
 
             @pl.when(cut > 0)
@@ -220,7 +224,7 @@
                 prime(True)
                 sweep(tile0, True)
 
-            @pl.when(cut == 0)
+            @pl.when((cut == 0) & (qt == 0))
             def _():
                 prime(False)
 
@@ -481,9 +485,7 @@
     out_ref[at : at + 16] = tail.astype(BF)
     at += 16
     gwk = jnp.concatenate(pieces[parts + 1 : parts + 1 + half // 16], axis=0)
-    hi = gwk.astype(BF)
-    out_ref[at : at + half] = hi
-    out_ref[at + half : at + 2 * half] = (gwk - hi.astype(F32)).astype(BF)
+    out_ref[at : at + half] = gwk.astype(BF)
 
 
 def last_kernel(
@@ -509,7 +511,7 @@
     for h in range(heads):
         gwq_ref[h] = gathered(h * half, half)
     at = heads * half
-    gwk_ref[...] = gathered(at + rows + 16, half) + gathered(at + rows + 16 + half, half)
+    gwk_ref[...] = gathered(at + rows + 16, half)
     adj_ref[...] = jnp.zeros_like(adj_ref)
     adjs_ref[...] = jnp.zeros_like(adjs_ref)
 
@@ -664,7 +666,7 @@
         arrived.append(
             lax.ppermute(pieces[k], "tensor", [(i, (i + k) % tensor) for i in range(tensor)])
         )
-    packed = heads * half + rows + 16 + 2 * half
+    packed = heads * half + rows + 16 + half
     part, out = pl.pallas_call(
         functools.partial(join_kernel, tensor),
         out_shape=(sds((rows, n), F32), sds((packed, width), BF)),

time: 76.6 us -> 76.2 us (level)
  no operation moved by 1% of the time
where the time goes in v3:
time: 76.2 us; the launch traced here: 75.9 us
  waiting for transfers between devices  23 us (30%)
  Pallas kernels  17.3 us (23%)
  starting transfers between devices  16.5 us (22%)
  blocking collectives  14.8 us (19%)
  other arithmetic  2.43 us (3%)
  local copies, waits for them, and re-layouts  1.03 us (1%)
  between operations  0.81 us (1%)
    ppermute x2, waiting for transfers between devices, hop(): lax.ppermute(x, 'seq', [(i, i + distance) for i in everyone if i + distan...  18.6 us
    all_gather x1, blocking collectives, shards(): gathered = lax.all_gather(out, 'seq')  14.8 us
    ppermute x2, starting transfers between devices, hop(): lax.ppermute(x, 'seq', [(i, i + distance) for i in everyone if i + distan...  8.33 us
    ppermute x3, starting transfers between devices, shards(): lax.ppermute(pieces[k], 'tensor', [(i, (i + k) % tensor) for i in range(t...  5.57 us
    pallas_call x1, Pallas kernels, shards(): pl.pallas_call(functools.partial(main_kernel, scale, 2.0 / (n * seq), flo...  5.19 us
    pallas_call x1, Pallas kernels, shards(): pl.pallas_call(student_kernel, out_shape=(wide, sds((width, n), F32), wid...  4.87 us
    ppermute x3, waiting for transfers between devices, shards(): lax.ppermute(pieces[k], 'tensor', [(i, (i + k) % tensor) for i in range(t...  4.36 us
    pallas_call x1, Pallas kernels, shards(): pl.pallas_call(functools.partial(teacher_kernel, scale), out_shape=(sds((...  3.85 us
  transfers between devices with their start and end apart: 8, of which 4 were waited for; matrix products, arithmetic and copies ran while one was open for 2% of the time, Pallas kernels for 13%

profile of v3, /device:TPU:0, one launch (start us, length us, event | category | flops | bytes accessed | tf_op | source)
XLA Modules:
  0.0 75.9 jit_solution(8302876003650450270)
XLA Ops:
  0.6 0.0 copy-start.5
  0.6 0.8 fusion.2
  1.4 1.1 %fusion.1 = bf16[2064,128]{1,0:T(8,128)(2,1)S(1)} fusion(bf16[8,128]{1,0:T(8,128)(2,1)S(1)} %fusion.2, bf16[1024,128]{1,0:T(8,128)(2,1)} %v_ref.5, bf16[1024,128]{1,0:T(8,128)(2,1)} %k_ref.5), kind=kLoop, calls=%fused_computation.3 | loop fusion | flops 2113536 | bytes 1054720 | tf_op jit(solution)/shard_map/concatenate | solution.py:561
  2.5 4.9 %collective-permute-start.1 = (bf16[2064,128]{1,0:T(8,128)(2,1)S(1)}, bf16[2064,128]{1,0:T(8,128)(2,1)S(1)}, u32[]{:S(2)}, u32[]{:S(2)}) collective-permute-start(bf16[2064,128]{1,0:T(8,128)(2,1)S(1)} %fusion.1), channel_id=1, source_target_pairs={{0,8},{4,12},{8,16},{12,20},{16,24},{20,28},{1,9},{5,13},{9,17},{1... | collective-permute-start | bytes 1585160 | tf_op jit(solution)/shard_map/ppermute | solution.py:564
  7.4 3.4 %collective-permute-start.3 = (bf16[2064,128]{1,0:T(8,128)(2,1)S(1)}, bf16[2064,128]{1,0:T(8,128)(2,1)S(1)}, u32[]{:S(2)}, u32[]{:S(2)}) collective-permute-start(bf16[2064,128]{1,0:T(8,128)(2,1)S(1)} %fusion.1), channel_id=1, source_target_pairs={{0,16},{4,20},{8,24},{12,28},{1,17},{5,21},{9,25},{13,29},{2,18},{... | collective-permute-start | bytes 1585160 | tf_op jit(solution)/shard_map/ppermute | solution.py:564
  10.9 1.3 %collective-permute-start = (bf16[2064,128]{1,0:T(8,128)(2,1)S(1)}, bf16[2064,128]{1,0:T(8,128)(2,1)S(1)}, u32[]{:S(2)}, u32[]{:S(2)}) collective-permute-start(bf16[2064,128]{1,0:T(8,128)(2,1)S(1)} %fusion.1), channel_id=1, source_target_pairs={{0,4},{8,12},{16,20},{24,28},{1,5},{9,13},{17,21},{25,29},{2,6},{1... | collective-permute-start | bytes 1585160 | tf_op jit(solution)/shard_map/ppermute | solution.py:567
  12.2 6.5 %collective-permute-done.1.two_ref = bf16[2064,128]{1,0:T(8,128)(2,1)S(1)} collective-permute-done((bf16[2064,128]{1,0:T(8,128)(2,1)S(1)}, bf16[2064,128]{1,0:T(8,128)(2,1)S(1)}, u32[]{:S(2)}, u32[]{:S(2)}) %collective-permute-start.1) | collective-permute-done | bytes 528416 | tf_op jit(solution)/shard_map/ppermute | solution.py:564
  18.7 0.0 collective-permute-start.2
  18.7 0.0 copy-done.5
  18.7 0.1 copy.12
  18.8 12.2 %collective-permute-done.3.four_ref = bf16[2064,128]{1,0:T(8,128)(2,1)S(1)} collective-permute-done((bf16[2064,128]{1,0:T(8,128)(2,1)S(1)}, bf16[2064,128]{1,0:T(8,128)(2,1)S(1)}, u32[]{:S(2)}, u32[]{:S(2)}) %collective-permute-start.3) | collective-permute-done | bytes 528416 | tf_op jit(solution)/shard_map/ppermute | solution.py:564
  30.9 1.3 %collective-permute-start.4 = (bf16[2064,128]{1,0:T(8,128)(2,1)S(1)}, bf16[2064,128]{1,0:T(8,128)(2,1)S(1)}, u32[]{:S(2)}, u32[]{:S(2)}) collective-permute-start(bf16[2064,128]{1,0:T(8,128)(2,1)S(1)} %collective-permute-done.3.four_ref), channel_id=1, source_target_pairs={{4,0},{12,8},{20,16},{28,24},{5,1},{13,9},{21,17},{29,25},{6,2},{1... | collective-permute-start | bytes 1585160 | tf_op jit(solution)/shard_map/ppermute | solution.py:626
  32.2 0.6 convert_reduce_fusion.edge_ref
  32.8 0.0 copy-start.3
  32.8 0.0 copy-start.4
  32.8 3.9 %shard_map.93 = (bf16[128,1024]{1,0:T(8,128)(2,1)S(1)}, f32[128,2048]{1,0:T(8,128)S(1)}, f32[8,2048]{1,0:T(8,128)S(1)}) custom-call(bf16[1024,256]{1,0:T(8,128)(2,1)S(1)} %bitcast.14, bf16[1024,128]{1,0:T(8,128)(2,1)S(1)} %copy-done.1, bf16[1024,128]{1,0:T(8,128)(2,1)S(1)} %copy-done, s32[1,1024]{1,0:T(1,128)S(1)} %bitcast.18), custom_call_target="tpu_custom_call" | custom-call | flops 1073741824 | bytes 4194304 | tf_op jit(solution)/shard_map/pallas_call | solution.py:589
  36.7 4.9 %shard_map.94 = (f32[128,2048]{1,0:T(8,128)S(1)}, f32[128,1024]{1,0:T(8,128)S(1)}, f32[128,2048]{1,0:T(8,128)S(1)}, f32[8,2048]{1,0:T(8,128)S(1)}) custom-call(bf16[1024,256]{1,0:T(8,128)(2,1)S(1)} %bitcast.15, bf16[1024,128]{1,0:T(8,128)(2,1)S(1)} %copy-done.1, bf16[128,1024]{1,0:T(8,128)(2,1)S(1)} %get-tuple-element.27.vt_ref, s32[1,1024]{1,0:T(1,128)S(1)} %bitcast.19, ...), custom_call_target="tpu_custom_call" | custom-call | flops 1073741824 | bytes 4194304 | tf_op jit(solution)/shard_map/pallas_call | solution.py:598
  41.6 0.0 collective-permute-done.own_ref
  41.6 0.0 collective-permute-done.2.swap_two_ref
  41.6 1.0 %shard_map.95 = (f32[128,2048]{1,0:T(8,128)S(1)}, f32[8,2048]{1,0:T(8,128)S(1)}, f32[128,2048]{1,0:T(8,128)S(1)}, f32[128,128]{1,0:T(8,128)S(1)}, f32[128,128]{1,0:T(8,128)S(1)}) custom-call(s32[1024]{0:T(1024)S(1)} %copy-done.2, bf16[1024,256]{1,0:T(8,128)(2,1)S(1)} %bitcast.16, s32[1,1024]{1,0:T(1,128)S(1)} %bitcast.20, bf16[64,128]{1,0:T(8,128)(2,1)S(1)} %bitcast.24, ...), custom_call_target="tpu_custom_call" | custom-call | flops 2147483648 | bytes 4194304 | tf_op jit(solution)/shard_map/pallas_call | solution.py:609
  42.6 0.0 collective-permute-done.4.swap_four_ref
  42.6 5.2 %shard_map.96 = (bf16[1024,256]{1,0:T(8,128)(2,1)S(1)}, bf16[128,128]{1,0:T(8,128)(2,1)S(1)}, bf16[48,1024]{1,0:T(8,128)(2,1)S(1)}, bf16[48,1024]{1,0:T(8,128)(2...) custom-call(s32[1024]{0:T(1024)S(1)} %copy-done.2, bf16[1024,256]{1,0:T(8,128)(2,1)S(1)} %bitcast.17, ...), custom_call_target="tpu_custom_call" | custom-call | flops 4294967296 | bytes 8388608 | tf_op jit(solution)/shard_map/pallas_call | solution.py:627
  47.8 1.6 %collective-permute-start.5 = (bf16[48,1024]{1,0:T(8,128)(2,1)S(1)}, bf16[48,1024]{1,0:T(8,128)(2,1)S(1)}, u32[]{:S(2)}, u32[]{:S(2)}) collective-permute-start(bf16[48,1024]{1,0:T(8,128)(2,1)S(1)} %get-tuple-element.42), channel_id=1, source_target_pairs={{0,1},{1,2},{2,3},{3,0},{4,5},{5,6},{6,7},{7,4},{8,9},{9,10},{10,1... | collective-permute-start | bytes 294920 | tf_op jit(solution)/shard_map/ppermute | solution.py:667
  49.5 2.6 %collective-permute-start.6 = (bf16[48,1024]{1,0:T(8,128)(2,1)S(1)}, bf16[48,1024]{1,0:T(8,128)(2,1)S(1)}, u32[]{:S(2)}, u32[]{:S(2)}) collective-permute-start(bf16[48,1024]{1,0:T(8,128)(2,1)S(1)} %get-tuple-element.43), channel_id=1, source_target_pairs={{0,2},{1,3},{2,0},{3,1},{4,6},{5,7},{6,4},{7,5},{8,10},{9,11},{10,... | collective-permute-start | bytes 294920 | tf_op jit(solution)/shard_map/ppermute | solution.py:667
  52.0 1.4 %collective-permute-start.7 = (bf16[48,1024]{1,0:T(8,128)(2,1)S(1)}, bf16[48,1024]{1,0:T(8,128)(2,1)S(1)}, u32[]{:S(2)}, u32[]{:S(2)}) collective-permute-start(bf16[48,1024]{1,0:T(8,128)(2,1)S(1)} %get-tuple-element.44), channel_id=1, source_target_pairs={{0,3},{1,0},{2,1},{3,2},{4,7},{5,4},{6,5},{7,6},{8,11},{9,8},{10,9... | collective-permute-start | bytes 294920 | tf_op jit(solution)/shard_map/ppermute | solution.py:667
  53.4 0.9 %reshape.25 = bf16[1024,2,128]{2,1,0:T(2,128)(2,1)} reshape(bf16[1024,256]{1,0:T(8,128)(2,1)S(1)} %get-tuple-element.39) | data formatting | bytes 1048576 | tf_op jit(solution)/shard_map/reshape | solution.py:692
  54.3 0.0 collective-permute-done.5.refs_1_
  54.3 2.5 %collective-permute-done.6.refs_2_ = bf16[48,1024]{1,0:T(8,128)(2,1)S(1)} collective-permute-done((bf16[48,1024]{1,0:T(8,128)(2,1)S(1)}, bf16[48,1024]{1,0:T(8,128)(2,1)S(1)}, u32[]{:S(2)}, u32[]{:S(2)}) %collective-permute-start.6) | collective-permute-done | bytes 98336 | tf_op jit(solution)/shard_map/ppermute | solution.py:667
  56.9 1.8 %collective-permute-done.7.refs_3_ = bf16[48,1024]{1,0:T(8,128)(2,1)S(1)} collective-permute-done((bf16[48,1024]{1,0:T(8,128)(2,1)S(1)}, bf16[48,1024]{1,0:T(8,128)(2,1)S(1)}, u32[]{:S(2)}, u32[]{:S(2)}) %collective-permute-start.7) | collective-permute-done | bytes 98336 | tf_op jit(solution)/shard_map/ppermute | solution.py:667
  58.7 0.6 shard_map.97
  59.3 14.8 %all-gather = bf16[1920,128]{1,0:T(8,128)(2,1)S(1)} all-gather(bf16[240,128]{1,0:T(8,128)(2,1)S(1)} %get-tuple-element.45), channel_id=2, replica_groups=mesh['seq'=8,'tensor'=4] {'seq'}, dimensions={0}, use_global_device_ids=true | all-gather | bytes 552960 | tf_op jit(solution)/shard_map/all_gather | solution.py:678
  74.1 1.7 %shard_map.98 = (f32[32,1024]{1,0:T(8,128)}, f32[2,64,128]{2,1,0:T(8,128)}, f32[64,128]{1,0:T(8,128)}) custom-call(s32[1024]{0:T(1024)S(1)} %copy-done.2, s32[1024]{0:T(1024)S(1)} %convert_reduce_fusion.edge_ref, bf16[8,240,128]{2,1,0:T(8,128)(2,1)S(1)} %bitcast.13, f32[32,1024]{1,0:T(8,128)S(1)} %get-tuple-element.46.sum_ref, bf16[1024,128]{1,0:T(8,128)(2,1)S(1)} %copy-done), custom_call_target="tpu_custom_call" | custom-call | flops 67108864 | bytes 2097152 | tf_op jit(solution)/shard_map/pallas_call | solution.py:679
  (8 shorter events, 0.0 us)
Async XLA Ops:
  0.6 18.0 %copy-start.5 = (bf16[1024,2,128]{2,1,0:T(2,128)(2,1)S(1)}, bf16[1024,2,128]{2,1,0:T(2,128)(2,1)}, u32[]{:S(2)}) copy-start(bf16[1024,2,128]{2,1,0:T(2,128)(2,1)} %param.6) | copy-start | bytes 1572868
  1.4 30.8 %copy-start.2 = (s32[1024]{0:T(1024)S(1)}, s32[1024]{0:T(1024)}, u32[]{:S(2)}) copy-start(s32[1024]{0:T(1024)} %doc_ref.7) | copy-start | bytes 12292
  1.4 31.4 %copy-start = (bf16[1024,128]{1,0:T(8,128)(2,1)S(1)}, bf16[1024,128]{1,0:T(8,128)(2,1)}, u32[]{:S(2)}) copy-start(bf16[1024,128]{1,0:T(8,128)(2,1)} %v_ref.5) | copy-start | bytes 786436
  1.4 31.4 %copy-start.1 = (bf16[1024,128]{1,0:T(8,128)(2,1)S(1)}, bf16[1024,128]{1,0:T(8,128)(2,1)}, u32[]{:S(2)}) copy-start(bf16[1024,128]{1,0:T(8,128)(2,1)} %k_ref.5) | copy-start | bytes 786436
  2.5 16.1 %collective-permute-start.1 = (bf16[2064,128]{1,0:T(8,128)(2,1)S(1)}, bf16[2064,128]{1,0:T(8,128)(2,1)S(1)}, u32[]{:S(2)}, u32[]{:S(2)}) collective-permute-start(bf16[2064,128]{1,0:T(8,128)(2,1)S(1)} %fusion.1), channel_id=1, source_target_pairs={{0,8},{4,12},{8,16},{12,20},{16,24},{20,28},{1,9},{5,13},{9,17},{1... | collective-permute-start | bytes 1585160 | tf_op jit(solution)/shard_map/ppermute | solution.py:564
  7.4 23.5 %collective-permute-start.3 = (bf16[2064,128]{1,0:T(8,128)(2,1)S(1)}, bf16[2064,128]{1,0:T(8,128)(2,1)S(1)}, u32[]{:S(2)}, u32[]{:S(2)}) collective-permute-start(bf16[2064,128]{1,0:T(8,128)(2,1)S(1)} %fusion.1), channel_id=1, source_target_pairs={{0,16},{4,20},{8,24},{12,28},{1,17},{5,21},{9,25},{13,29},{2,18},{... | collective-permute-start | bytes 1585160 | tf_op jit(solution)/shard_map/ppermute | solution.py:564
  10.9 30.7 %collective-permute-start = (bf16[2064,128]{1,0:T(8,128)(2,1)S(1)}, bf16[2064,128]{1,0:T(8,128)(2,1)S(1)}, u32[]{:S(2)}, u32[]{:S(2)}) collective-permute-start(bf16[2064,128]{1,0:T(8,128)(2,1)S(1)} %fusion.1), channel_id=1, source_target_pairs={{0,4},{8,12},{16,20},{24,28},{1,5},{9,13},{17,21},{25,29},{2,6},{1... | collective-permute-start | bytes 1585160 | tf_op jit(solution)/shard_map/ppermute | solution.py:567
  18.7 22.9 %collective-permute-start.2 = (bf16[2064,128]{1,0:T(8,128)(2,1)S(1)}, bf16[2064,128]{1,0:T(8,128)(2,1)S(1)}, u32[]{:S(2)}, u32[]{:S(2)}) collective-permute-start(bf16[2064,128]{1,0:T(8,128)(2,1)S(1)} %collective-permute-done.1.two_ref), channel_id=1, source_target_pairs={{0,4},{4,0},{8,12},{12,8},{16,20},{20,16},{24,28},{28,24},{1,5},{5... | collective-permute-start | bytes 1585160 | tf_op jit(solution)/shard_map/ppermute | solution.py:608
  30.9 11.7 %collective-permute-start.4 = (bf16[2064,128]{1,0:T(8,128)(2,1)S(1)}, bf16[2064,128]{1,0:T(8,128)(2,1)S(1)}, u32[]{:S(2)}, u32[]{:S(2)}) collective-permute-start(bf16[2064,128]{1,0:T(8,128)(2,1)S(1)} %collective-permute-done.3.four_ref), channel_id=1, source_target_pairs={{4,0},{12,8},{20,16},{28,24},{5,1},{13,9},{21,17},{29,25},{6,2},{1... | collective-permute-start | bytes 1585160 | tf_op jit(solution)/shard_map/ppermute | solution.py:626
  32.8 3.9 %copy-start.3 = (bf16[2,128,64]{1,2,0:T(8,128)(2,1)S(1)}, bf16[2,128,64]{1,2,0:T(8,128)(2,1)}, u32[]{:S(2)}) copy-start(bf16[2,128,64]{1,2,0:T(8,128)(2,1)} %param.10) | copy-start | bytes 98308
  32.8 3.9 %copy-start.4 = (bf16[128,64]{0,1:T(8,128)(2,1)S(1)}, bf16[128,64]{0,1:T(8,128)(2,1)}, u32[]{:S(2)}) copy-start(bf16[128,64]{0,1:T(8,128)(2,1)} %param.11) | copy-start | bytes 49156
  47.8 6.5 %collective-permute-start.5 = (bf16[48,1024]{1,0:T(8,128)(2,1)S(1)}, bf16[48,1024]{1,0:T(8,128)(2,1)S(1)}, u32[]{:S(2)}, u32[]{:S(2)}) collective-permute-start(bf16[48,1024]{1,0:T(8,128)(2,1)S(1)} %get-tuple-element.42), channel_id=1, source_target_pairs={{0,1},{1,2},{2,3},{3,0},{4,5},{5,6},{6,7},{7,4},{8,9},{9,10},{10,1... | collective-permute-start | bytes 294920 | tf_op jit(solution)/shard_map/ppermute | solution.py:667
  49.5 7.4 %collective-permute-start.6 = (bf16[48,1024]{1,0:T(8,128)(2,1)S(1)}, bf16[48,1024]{1,0:T(8,128)(2,1)S(1)}, u32[]{:S(2)}, u32[]{:S(2)}) collective-permute-start(bf16[48,1024]{1,0:T(8,128)(2,1)S(1)} %get-tuple-element.43), channel_id=1, source_target_pairs={{0,2},{1,3},{2,0},{3,1},{4,6},{5,7},{6,4},{7,5},{8,10},{9,11},{10,... | collective-permute-start | bytes 294920 | tf_op jit(solution)/shard_map/ppermute | solution.py:667
  52.0 6.6 %collective-permute-start.7 = (bf16[48,1024]{1,0:T(8,128)(2,1)S(1)}, bf16[48,1024]{1,0:T(8,128)(2,1)S(1)}, u32[]{:S(2)}, u32[]{:S(2)}) collective-permute-start(bf16[48,1024]{1,0:T(8,128)(2,1)S(1)} %get-tuple-element.44), channel_id=1, source_target_pairs={{0,3},{1,0},{2,1},{3,2},{4,7},{5,4},{6,5},{7,6},{8,11},{9,8},{10,9... | collective-permute-start | bytes 294920 | tf_op jit(solution)/shard_map/ppermute | solution.py:667

commit v4 on v3

--- a/solution.py
+++ b/solution.py
@@ -15,7 +15,7 @@
 TK = 1024
 TC = 256
 CH = 512
-CHAINS = 4
+CHAINS = 8
 BF = jnp.bfloat16
 F32 = jnp.float32
 
@@ -126,6 +126,27 @@
         c.wait()
 
 
+def tile_rows(kt):
+    if isinstance(kt, int):
+        return pl.ds(kt * TK, TK)
+    return pl.ds(pl.multiple_of(kt * TK, TK), TK)
+
+
+def each_tile(begin_key, size, body):
+    if size != 2 * TK:
+        lax.fori_loop(begin_key // TK, size // TK, lambda kt, carry: body(kt) or carry, 0)
+        return
+
+    @pl.when(begin_key < TK)
+    def _():
+        body(0)
+        body(1)
+
+    @pl.when((begin_key >= TK) & (begin_key < size))
+    def _():
+        body(1)
+
+
 def matching(codes, code):
     return jnp.sum((codes[...].astype(F32) == code).astype(jnp.int32))
 
@@ -142,8 +163,8 @@
 
     @pl.when(begin_key < stop_key)
     def _():
-        def prepare(kt, carry):
-            row = pl.ds(pl.multiple_of(kt * TK, TK), TK)
+        def prepare(kt):
+            row = tile_rows(kt)
             kf = feature_t(mm(wk_ref[...], wink[row], NT))
             wkf[:, row] = kf
             j = lax.broadcasted_iota(jnp.int32, (1, TK), 1) + kt * TK
@@ -154,9 +175,8 @@
             part = kfm.astype(F32)
             for c in range(TK // 128):
                 csum_ref[...] += part[:, c * 128 : (c + 1) * 128]
-            return carry
-
-        lax.fori_loop(tile0, tiles, prepare, 0)
+
+        each_tile(begin_key, stop_key, prepare)
         key = lax.broadcasted_iota(jnp.int32, bias_ref.shape, 0) + tile0 * TK
         bias_ref[...] = jnp.where(key >= begin_key, 0.0, NEG)
         wq = min(n, CHAINS * TC // heads)
@@ -424,16 +444,15 @@
     adjs_col = adj_ref[:, width : width + 1] + adj_ref[:, width + 1 : width + 2]
 
     def back_over(begin_key, stop_key, keys, values, feats):
-        def back(kt, carry):
-            row = pl.ds(pl.multiple_of(kt * TK, TK), TK)
+        def back(kt):
+            row = tile_rows(kt)
             more = mm(adj_b, values[row], NT) + adjs_col
             j = lax.broadcasted_iota(jnp.int32, (1, TK), 1) + kt * TK
             gl = feature_back_t(feats[:, row], more)
             gl = jnp.where(j >= begin_key, gl, 0.0).astype(BF)
             gwk_ref[...] += mm(gl, keys[row])
-            return carry
-
-        lax.fori_loop(begin_key // TK, stop_key // TK, back, 0)
+
+        each_tile(begin_key, stop_key, back)
 
     for slot in range(2):
         finish(load(two_ref, slot, neark, nearv, nearc, near_sem)[:2])

time: 76.2 us -> 76.5 us (level)
  blocking collectives: 14.8 us -> 16.9 us
  waiting for transfers between devices: 23 us -> 21.3 us
    all_gather x1, blocking collectives: 14.8 us -> 16.9 us  [shards(): gathered = lax.all_gather(out, 'seq')]
    ppermute x3, waiting for transfers between devices: 4.36 us -> 2.66 us  [shards(): lax.ppermute(pieces[k], 'tensor', [(i, (i + k) % tensor) for i in range(t...]
where the time goes in v4:
time: 76.5 us; the launch traced here: 76.3 us
  waiting for transfers between devices  21.3 us (28%)
  Pallas kernels  17.4 us (23%)
  blocking collectives  16.9 us (22%)
  starting transfers between devices  16.5 us (22%)
  other arithmetic  2.43 us (3%)
  local copies, waits for them, and re-layouts  1.03 us (1%)
  between operations  0.81 us (1%)
    ppermute x2, waiting for transfers between devices, hop(): lax.ppermute(x, 'seq', [(i, i + distance) for i in everyone if i + distan...  18.6 us
    all_gather x1, blocking collectives, shards(): gathered = lax.all_gather(out, 'seq')  16.9 us
    ppermute x2, starting transfers between devices, hop(): lax.ppermute(x, 'seq', [(i, i + distance) for i in everyone if i + distan...  8.33 us
    ppermute x3, starting transfers between devices, shards(): lax.ppermute(pieces[k], 'tensor', [(i, (i + k) % tensor) for i in range(t...  5.57 us
    pallas_call x1, Pallas kernels, shards(): pl.pallas_call(functools.partial(main_kernel, scale, 2.0 / (n * seq), flo...  5.24 us
    pallas_call x1, Pallas kernels, shards(): pl.pallas_call(student_kernel, out_shape=(wide, sds((width, n), F32), wid...  4.87 us
    pallas_call x1, Pallas kernels, shards(): pl.pallas_call(functools.partial(teacher_kernel, scale), out_shape=(sds((...  3.85 us
    ppermute x3, waiting for transfers between devices, shards(): lax.ppermute(pieces[k], 'tensor', [(i, (i + k) % tensor) for i in range(t...  2.66 us
  transfers between devices with their start and end apart: 8, of which 4 were waited for; matrix products, arithmetic and copies ran while one was open for 2% of the time, Pallas kernels for 13%

profile of v4, /device:TPU:0, one launch (start us, length us, event | category | flops | bytes accessed | tf_op | source)
XLA Modules:
  0.0 76.3 jit_solution(4259194025603561490)
XLA Ops:
  0.6 0.0 copy-start.5
  0.6 0.8 fusion.2
  1.4 1.1 %fusion.1 = bf16[2064,128]{1,0:T(8,128)(2,1)S(1)} fusion(bf16[8,128]{1,0:T(8,128)(2,1)S(1)} %fusion.2, bf16[1024,128]{1,0:T(8,128)(2,1)} %v_ref.5, bf16[1024,128]{1,0:T(8,128)(2,1)} %k_ref.5), kind=kLoop, calls=%fused_computation.3 | loop fusion | flops 2113536 | bytes 1054720 | tf_op jit(solution)/shard_map/concatenate | solution.py:580
  2.5 4.9 %collective-permute-start.1 = (bf16[2064,128]{1,0:T(8,128)(2,1)S(1)}, bf16[2064,128]{1,0:T(8,128)(2,1)S(1)}, u32[]{:S(2)}, u32[]{:S(2)}) collective-permute-start(bf16[2064,128]{1,0:T(8,128)(2,1)S(1)} %fusion.1), channel_id=1, source_target_pairs={{0,8},{4,12},{8,16},{12,20},{16,24},{20,28},{1,9},{5,13},{9,17},{1... | collective-permute-start | bytes 1585160 | tf_op jit(solution)/shard_map/ppermute | solution.py:583
  7.4 3.4 %collective-permute-start.3 = (bf16[2064,128]{1,0:T(8,128)(2,1)S(1)}, bf16[2064,128]{1,0:T(8,128)(2,1)S(1)}, u32[]{:S(2)}, u32[]{:S(2)}) collective-permute-start(bf16[2064,128]{1,0:T(8,128)(2,1)S(1)} %fusion.1), channel_id=1, source_target_pairs={{0,16},{4,20},{8,24},{12,28},{1,17},{5,21},{9,25},{13,29},{2,18},{... | collective-permute-start | bytes 1585160 | tf_op jit(solution)/shard_map/ppermute | solution.py:583
  10.9 1.3 %collective-permute-start = (bf16[2064,128]{1,0:T(8,128)(2,1)S(1)}, bf16[2064,128]{1,0:T(8,128)(2,1)S(1)}, u32[]{:S(2)}, u32[]{:S(2)}) collective-permute-start(bf16[2064,128]{1,0:T(8,128)(2,1)S(1)} %fusion.1), channel_id=1, source_target_pairs={{0,4},{8,12},{16,20},{24,28},{1,5},{9,13},{17,21},{25,29},{2,6},{1... | collective-permute-start | bytes 1585160 | tf_op jit(solution)/shard_map/ppermute | solution.py:586
  12.2 6.5 %collective-permute-done.1.two_ref = bf16[2064,128]{1,0:T(8,128)(2,1)S(1)} collective-permute-done((bf16[2064,128]{1,0:T(8,128)(2,1)S(1)}, bf16[2064,128]{1,0:T(8,128)(2,1)S(1)}, u32[]{:S(2)}, u32[]{:S(2)}) %collective-permute-start.1) | collective-permute-done | bytes 528416 | tf_op jit(solution)/shard_map/ppermute | solution.py:583
  18.7 0.0 collective-permute-start.2
  18.7 0.0 copy-done.5
  18.7 0.1 copy.12
  18.8 12.2 %collective-permute-done.3.four_ref = bf16[2064,128]{1,0:T(8,128)(2,1)S(1)} collective-permute-done((bf16[2064,128]{1,0:T(8,128)(2,1)S(1)}, bf16[2064,128]{1,0:T(8,128)(2,1)S(1)}, u32[]{:S(2)}, u32[]{:S(2)}) %collective-permute-start.3) | collective-permute-done | bytes 528416 | tf_op jit(solution)/shard_map/ppermute | solution.py:583
  30.9 1.3 %collective-permute-start.4 = (bf16[2064,128]{1,0:T(8,128)(2,1)S(1)}, bf16[2064,128]{1,0:T(8,128)(2,1)S(1)}, u32[]{:S(2)}, u32[]{:S(2)}) collective-permute-start(bf16[2064,128]{1,0:T(8,128)(2,1)S(1)} %collective-permute-done.3.four_ref), channel_id=1, source_target_pairs={{4,0},{12,8},{20,16},{28,24},{5,1},{13,9},{21,17},{29,25},{6,2},{1... | collective-permute-start | bytes 1585160 | tf_op jit(solution)/shard_map/ppermute | solution.py:645
  32.2 0.6 convert_reduce_fusion.edge_ref
  32.8 0.0 copy-start.3
  32.8 0.0 copy-start.4
  32.8 3.9 %shard_map.93 = (bf16[128,1024]{1,0:T(8,128)(2,1)S(1)}, f32[128,2048]{1,0:T(8,128)S(1)}, f32[8,2048]{1,0:T(8,128)S(1)}) custom-call(bf16[1024,256]{1,0:T(8,128)(2,1)S(1)} %bitcast.14, bf16[1024,128]{1,0:T(8,128)(2,1)S(1)} %copy-done.1, bf16[1024,128]{1,0:T(8,128)(2,1)S(1)} %copy-done, s32[1,1024]{1,0:T(1,128)S(1)} %bitcast.18), custom_call_target="tpu_custom_call" | custom-call | flops 1073741824 | bytes 4194304 | tf_op jit(solution)/shard_map/pallas_call | solution.py:608
  36.7 4.9 %shard_map.94 = (f32[128,2048]{1,0:T(8,128)S(1)}, f32[128,1024]{1,0:T(8,128)S(1)}, f32[128,2048]{1,0:T(8,128)S(1)}, f32[8,2048]{1,0:T(8,128)S(1)}) custom-call(bf16[1024,256]{1,0:T(8,128)(2,1)S(1)} %bitcast.15, bf16[1024,128]{1,0:T(8,128)(2,1)S(1)} %copy-done.1, bf16[128,1024]{1,0:T(8,128)(2,1)S(1)} %get-tuple-element.27.vt_ref, s32[1,1024]{1,0:T(1,128)S(1)} %bitcast.19, ...), custom_call_target="tpu_custom_call" | custom-call | flops 1073741824 | bytes 4194304 | tf_op jit(solution)/shard_map/pallas_call | solution.py:617
  41.6 0.0 collective-permute-done.own_ref
  41.6 0.0 collective-permute-done.2.swap_two_ref
  41.6 1.0 %shard_map.95 = (f32[128,2048]{1,0:T(8,128)S(1)}, f32[8,2048]{1,0:T(8,128)S(1)}, f32[128,2048]{1,0:T(8,128)S(1)}, f32[128,128]{1,0:T(8,128)S(1)}, f32[128,128]{1,0:T(8,128)S(1)}) custom-call(s32[1024]{0:T(1024)S(1)} %copy-done.2, bf16[1024,256]{1,0:T(8,128)(2,1)S(1)} %bitcast.16, s32[1,1024]{1,0:T(1,128)S(1)} %bitcast.20, bf16[64,128]{1,0:T(8,128)(2,1)S(1)} %bitcast.24, ...), custom_call_target="tpu_custom_call" | custom-call | flops 2147483648 | bytes 4194304 | tf_op jit(solution)/shard_map/pallas_call | solution.py:628
  42.6 0.0 collective-permute-done.4.swap_four_ref
  42.6 5.2 %shard_map.96 = (bf16[1024,256]{1,0:T(8,128)(2,1)S(1)}, bf16[128,128]{1,0:T(8,128)(2,1)S(1)}, bf16[48,1024]{1,0:T(8,128)(2,1)S(1)}, bf16[48,1024]{1,0:T(8,128)(2...) custom-call(s32[1024]{0:T(1024)S(1)} %copy-done.2, bf16[1024,256]{1,0:T(8,128)(2,1)S(1)} %bitcast.17, ...), custom_call_target="tpu_custom_call" | custom-call | flops 4294967296 | bytes 8388608 | tf_op jit(solution)/shard_map/pallas_call | solution.py:646
  47.9 1.6 %collective-permute-start.5 = (bf16[48,1024]{1,0:T(8,128)(2,1)S(1)}, bf16[48,1024]{1,0:T(8,128)(2,1)S(1)}, u32[]{:S(2)}, u32[]{:S(2)}) collective-permute-start(bf16[48,1024]{1,0:T(8,128)(2,1)S(1)} %get-tuple-element.42), channel_id=1, source_target_pairs={{0,1},{1,2},{2,3},{3,0},{4,5},{5,6},{6,7},{7,4},{8,9},{9,10},{10,1... | collective-permute-start | bytes 294920 | tf_op jit(solution)/shard_map/ppermute | solution.py:686
  49.5 2.6 %collective-permute-start.6 = (bf16[48,1024]{1,0:T(8,128)(2,1)S(1)}, bf16[48,1024]{1,0:T(8,128)(2,1)S(1)}, u32[]{:S(2)}, u32[]{:S(2)}) collective-permute-start(bf16[48,1024]{1,0:T(8,128)(2,1)S(1)} %get-tuple-element.43), channel_id=1, source_target_pairs={{0,2},{1,3},{2,0},{3,1},{4,6},{5,7},{6,4},{7,5},{8,10},{9,11},{10,... | collective-permute-start | bytes 294920 | tf_op jit(solution)/shard_map/ppermute | solution.py:686
  52.1 1.4 %collective-permute-start.7 = (bf16[48,1024]{1,0:T(8,128)(2,1)S(1)}, bf16[48,1024]{1,0:T(8,128)(2,1)S(1)}, u32[]{:S(2)}, u32[]{:S(2)}) collective-permute-start(bf16[48,1024]{1,0:T(8,128)(2,1)S(1)} %get-tuple-element.44), channel_id=1, source_target_pairs={{0,3},{1,0},{2,1},{3,2},{4,7},{5,4},{6,5},{7,6},{8,11},{9,8},{10,9... | collective-permute-start | bytes 294920 | tf_op jit(solution)/shard_map/ppermute | solution.py:686
  53.5 0.9 %reshape.25 = bf16[1024,2,128]{2,1,0:T(2,128)(2,1)} reshape(bf16[1024,256]{1,0:T(8,128)(2,1)S(1)} %get-tuple-element.39) | data formatting | bytes 1048576 | tf_op jit(solution)/shard_map/reshape | solution.py:711
  54.4 0.0 collective-permute-done.5.refs_1_
  54.4 2.2 %collective-permute-done.6.refs_2_ = bf16[48,1024]{1,0:T(8,128)(2,1)S(1)} collective-permute-done((bf16[48,1024]{1,0:T(8,128)(2,1)S(1)}, bf16[48,1024]{1,0:T(8,128)(2,1)S(1)}, u32[]{:S(2)}, u32[]{:S(2)}) %collective-permute-start.6) | collective-permute-done | bytes 98336 | tf_op jit(solution)/shard_map/ppermute | solution.py:686
  56.6 0.5 collective-permute-done.7.refs_3_
  57.0 0.6 shard_map.97
  57.7 16.9 %all-gather = bf16[1920,128]{1,0:T(8,128)(2,1)S(1)} all-gather(bf16[240,128]{1,0:T(8,128)(2,1)S(1)} %get-tuple-element.45), channel_id=2, replica_groups=mesh['seq'=8,'tensor'=4] {'seq'}, dimensions={0}, use_global_device_ids=true | all-gather | bytes 552960 | tf_op jit(solution)/shard_map/all_gather | solution.py:697
  74.6 1.7 %shard_map.98 = (f32[32,1024]{1,0:T(8,128)}, f32[2,64,128]{2,1,0:T(8,128)}, f32[64,128]{1,0:T(8,128)}) custom-call(s32[1024]{0:T(1024)S(1)} %copy-done.2, s32[1024]{0:T(1024)S(1)} %convert_reduce_fusion.edge_ref, bf16[8,240,128]{2,1,0:T(8,128)(2,1)S(1)} %bitcast.13, f32[32,1024]{1,0:T(8,128)S(1)} %get-tuple-element.46.sum_ref, bf16[1024,128]{1,0:T(8,128)(2,1)S(1)} %copy-done), custom_call_target="tpu_custom_call" | custom-call | flops 67108864 | bytes 2097152 | tf_op jit(solution)/shard_map/pallas_call | solution.py:698
  (8 shorter events, 0.0 us)
Async XLA Ops:
  0.6 18.0 %copy-start.5 = (bf16[1024,2,128]{2,1,0:T(2,128)(2,1)S(1)}, bf16[1024,2,128]{2,1,0:T(2,128)(2,1)}, u32[]{:S(2)}) copy-start(bf16[1024,2,128]{2,1,0:T(2,128)(2,1)} %param.6) | copy-start | bytes 1572868
  1.4 30.8 %copy-start.2 = (s32[1024]{0:T(1024)S(1)}, s32[1024]{0:T(1024)}, u32[]{:S(2)}) copy-start(s32[1024]{0:T(1024)} %doc_ref.7) | copy-start | bytes 12292
  1.4 31.4 %copy-start = (bf16[1024,128]{1,0:T(8,128)(2,1)S(1)}, bf16[1024,128]{1,0:T(8,128)(2,1)}, u32[]{:S(2)}) copy-start(bf16[1024,128]{1,0:T(8,128)(2,1)} %v_ref.5) | copy-start | bytes 786436
  1.4 31.4 %copy-start.1 = (bf16[1024,128]{1,0:T(8,128)(2,1)S(1)}, bf16[1024,128]{1,0:T(8,128)(2,1)}, u32[]{:S(2)}) copy-start(bf16[1024,128]{1,0:T(8,128)(2,1)} %k_ref.5) | copy-start | bytes 786436
  2.5 16.1 %collective-permute-start.1 = (bf16[2064,128]{1,0:T(8,128)(2,1)S(1)}, bf16[2064,128]{1,0:T(8,128)(2,1)S(1)}, u32[]{:S(2)}, u32[]{:S(2)}) collective-permute-start(bf16[2064,128]{1,0:T(8,128)(2,1)S(1)} %fusion.1), channel_id=1, source_target_pairs={{0,8},{4,12},{8,16},{12,20},{16,24},{20,28},{1,9},{5,13},{9,17},{1... | collective-permute-start | bytes 1585160 | tf_op jit(solution)/shard_map/ppermute | solution.py:583
  7.4 23.5 %collective-permute-start.3 = (bf16[2064,128]{1,0:T(8,128)(2,1)S(1)}, bf16[2064,128]{1,0:T(8,128)(2,1)S(1)}, u32[]{:S(2)}, u32[]{:S(2)}) collective-permute-start(bf16[2064,128]{1,0:T(8,128)(2,1)S(1)} %fusion.1), channel_id=1, source_target_pairs={{0,16},{4,20},{8,24},{12,28},{1,17},{5,21},{9,25},{13,29},{2,18},{... | collective-permute-start | bytes 1585160 | tf_op jit(solution)/shard_map/ppermute | solution.py:583
  10.9 30.7 %collective-permute-start = (bf16[2064,128]{1,0:T(8,128)(2,1)S(1)}, bf16[2064,128]{1,0:T(8,128)(2,1)S(1)}, u32[]{:S(2)}, u32[]{:S(2)}) collective-permute-start(bf16[2064,128]{1,0:T(8,128)(2,1)S(1)} %fusion.1), channel_id=1, source_target_pairs={{0,4},{8,12},{16,20},{24,28},{1,5},{9,13},{17,21},{25,29},{2,6},{1... | collective-permute-start | bytes 1585160 | tf_op jit(solution)/shard_map/ppermute | solution.py:586
  18.7 22.9 %collective-permute-start.2 = (bf16[2064,128]{1,0:T(8,128)(2,1)S(1)}, bf16[2064,128]{1,0:T(8,128)(2,1)S(1)}, u32[]{:S(2)}, u32[]{:S(2)}) collective-permute-start(bf16[2064,128]{1,0:T(8,128)(2,1)S(1)} %collective-permute-done.1.two_ref), channel_id=1, source_target_pairs={{0,4},{4,0},{8,12},{12,8},{16,20},{20,16},{24,28},{28,24},{1,5},{5... | collective-permute-start | bytes 1585160 | tf_op jit(solution)/shard_map/ppermute | solution.py:627
  30.9 11.7 %collective-permute-start.4 = (bf16[2064,128]{1,0:T(8,128)(2,1)S(1)}, bf16[2064,128]{1,0:T(8,128)(2,1)S(1)}, u32[]{:S(2)}, u32[]{:S(2)}) collective-permute-start(bf16[2064,128]{1,0:T(8,128)(2,1)S(1)} %collective-permute-done.3.four_ref), channel_id=1, source_target_pairs={{4,0},{12,8},{20,16},{28,24},{5,1},{13,9},{21,17},{29,25},{6,2},{1... | collective-permute-start | bytes 1585160 | tf_op jit(solution)/shard_map/ppermute | solution.py:645
  32.8 3.9 %copy-start.3 = (bf16[2,128,64]{1,2,0:T(8,128)(2,1)S(1)}, bf16[2,128,64]{1,2,0:T(8,128)(2,1)}, u32[]{:S(2)}) copy-start(bf16[2,128,64]{1,2,0:T(8,128)(2,1)} %param.10) | copy-start | bytes 98308
  32.8 3.9 %copy-start.4 = (bf16[128,64]{0,1:T(8,128)(2,1)S(1)}, bf16[128,64]{0,1:T(8,128)(2,1)}, u32[]{:S(2)}) copy-start(bf16[128,64]{0,1:T(8,128)(2,1)} %param.11) | copy-start | bytes 49156
  47.9 6.5 %collective-permute-start.5 = (bf16[48,1024]{1,0:T(8,128)(2,1)S(1)}, bf16[48,1024]{1,0:T(8,128)(2,1)S(1)}, u32[]{:S(2)}, u32[]{:S(2)}) collective-permute-start(bf16[48,1024]{1,0:T(8,128)(2,1)S(1)} %get-tuple-element.42), channel_id=1, source_target_pairs={{0,1},{1,2},{2,3},{3,0},{4,5},{5,6},{6,7},{7,4},{8,9},{9,10},{10,1... | collective-permute-start | bytes 294920 | tf_op jit(solution)/shard_map/ppermute | solution.py:686
  49.5 7.0 %collective-permute-start.6 = (bf16[48,1024]{1,0:T(8,128)(2,1)S(1)}, bf16[48,1024]{1,0:T(8,128)(2,1)S(1)}, u32[]{:S(2)}, u32[]{:S(2)}) collective-permute-start(bf16[48,1024]{1,0:T(8,128)(2,1)S(1)} %get-tuple-element.43), channel_id=1, source_target_pairs={{0,2},{1,3},{2,0},{3,1},{4,6},{5,7},{6,4},{7,5},{8,10},{9,11},{10,... | collective-permute-start | bytes 294920 | tf_op jit(solution)/shard_map/ppermute | solution.py:686
  52.1 4.9 %collective-permute-start.7 = (bf16[48,1024]{1,0:T(8,128)(2,1)S(1)}, bf16[48,1024]{1,0:T(8,128)(2,1)S(1)}, u32[]{:S(2)}, u32[]{:S(2)}) collective-permute-start(bf16[48,1024]{1,0:T(8,128)(2,1)S(1)} %get-tuple-element.44), channel_id=1, source_target_pairs={{0,3},{1,0},{2,1},{3,2},{4,7},{5,4},{6,5},{7,6},{8,11},{9,8},{10,9... | collective-permute-start | bytes 294920 | tf_op jit(solution)/shard_map/ppermute | solution.py:686
